TPU v7x, 128 devices: a whole 4x4x4 slice. The times are simulated.
128 devices in a mesh: task: 4 (over y), param: 32 (over z, x, core).
Axes of the slice: x: 4, y: 4, z: 4, core: 2. Of those that a mesh axis runs over, the one named last changes fastest.
Arguments:
- grads: bfloat16 [8, 8192, 4096], P('task', 'param')
- order: int32 [8], replicated, may hold values from 0 to 7, each once
Outputs:
- update: float32 [8192, 4096], P('param', 'task')
All inputs are finite; a program needn't handle non-finite values.
Results may differ from a plain program's by a relative error of at most 0.0003.
Values may be sent and summed in bfloat16 or wider, within the bound.
No kernel may reach another device: no remote copies, remote signals or barrier semaphores. Data moves between devices by JAX's collectives and lax.ppermute only.
A program may use at most 64 MiB of HBM per device.

v0:
```python
import functools

import jax
import jax.numpy as jnp
from jax import lax
from jax.sharding import Mesh
from jax.sharding import PartitionSpec as P

TASK_PARAM = ("task", "param_0", "param_1", "param_2")
PARAM = ("param_0", "param_1", "param_2")


def split_up(value, dim, devices):
    before, after = (value.shape[:dim], value.shape[dim + 1 :])
    return jnp.moveaxis(value.reshape(*before, devices, -1, *after), dim, 0)


def edges_of(length, count):
    unit = 8 if length >= 8 * count else 1
    return [length // unit * k // count * unit for k in range(1, count)]


def in_order(parts, dim):
    parts = jnp.moveaxis(parts, 0, dim)
    dims = parts.shape
    return parts.reshape(*dims[:dim], dims[dim] * dims[dim + 1], *dims[dim + 2 :])


def exchange_in_pieces(value, axis, pieces, split_dim, concat_dim):
    parts = split_up(value, split_dim, lax.axis_size(axis))
    cut = max(range(1, max(2, parts.ndim - 1)), key=lambda d: parts.shape[d])
    finished = []
    for slab in jnp.split(parts, edges_of(parts.shape[cut], pieces), axis=cut):
        if slab.size:
            finished.append(lax.all_to_all(slab, axis, split_axis=0, concat_axis=0, tiled=True))
    return in_order(jnp.concatenate(finished, axis=cut), concat_dim)


def by_axis(value, axes):
    return functools.reduce(lax.psum, axes, value)


def shards(grads, order):
    tasks_here, rows, width = grads.shape
    parts_task = lax.axis_size("task")
    total = tasks_here * parts_task
    block = width // parts_task
    mine = exchange_in_pieces(grads, "task", 2, 2, 0)
    flat = mine.reshape(total, -1)
    labels = jnp.arange(total, dtype=jnp.int32)
    coefs = jnp.eye(total, dtype=jnp.float32)
    local_gram = lax.dot_general(
        flat, flat, (((1,), (1,)), ((), ())), preferred_element_type=jnp.float32
    )
    gram = by_axis(local_gram, TASK_PARAM)
    for k in range(total):
        j = order[k]
        picked = (labels == j).astype(jnp.float32)
        column = jnp.sum(gram * picked[None, :], axis=1)
        d = jnp.sum(coefs * column[None, :], axis=1)
        norm_j = jnp.sum(column * picked)
        w = jnp.minimum(d, 0.0) / (norm_j + 1e-06)
        w = w * (1.0 - picked)
        coefs = coefs - w[:, None] * picked[None, :]
    weight = jnp.sum(coefs, axis=0)
    combined = jnp.zeros((rows, block), jnp.float32)
    for m in range(total):
        combined = combined + weight[m] * mine[m].astype(jnp.float32)
    energy = by_axis(jnp.sum(combined * combined), TASK_PARAM)
    entries = rows * lax.axis_size(PARAM) * width
    rms = jnp.sqrt(energy / entries + 1e-06)
    return combined * (0.5 / rms)


def solution(mesh):
    torus = Mesh(
        mesh.devices.reshape(mesh.shape["task"], 4, 4, 2), ("task", "param_0", "param_1", "param_2")
    )
    in_specs = (P("task", PARAM, None), P())
    out_specs = P(PARAM, "task")
    return jax.shard_map(
        shards, mesh=torus, in_specs=in_specs, out_specs=out_specs, check_vma=False
    )
```

profile of v0, /device:TPU:1, one launch (start us, length us, event | category | flops | bytes accessed | tf_op | source)
XLA Modules:
  0.0 167.1 jit_solution(2255050824678215293)
XLA Ops:
  0.0 2.6 %copy.7 = bf16[2,32,4,8,1024]{4,3,1,0,2:T(8,128)(2,1)S(1)} copy(bf16[2,32,4,8,1024]{4,3,2,1,0:T(8,128)(2,1)} %bitcast.35) | data formatting | bytes 8388608 | tf_op jit(solution)/shard_map/reshape | solution.py:15
  2.6 1.8 %fusion.8 = (bf16[4,2,128,1024]{3,2,1,0:T(8,128)(2,1)}, bf16[4,2,128,1024]{3,2,1,0:T(8,128)(2,1)S(1)}) fusion(bf16[4,2,256,1024]{3,2,1,0:T(8,128)(2,1)S(1)} %bitcast.34), kind=kLoop, calls=%fused_computation.63 | loop fusion | bytes 8388608 | tf_op jit(solution)/shard_map/split | solution.py:33
  4.4 30.5 %all_to_all.10 = bf16[4,2,128,1024]{3,2,1,0:T(8,128)(2,1)} all-to-all(bf16[4,2,128,1024]{3,2,1,0:T(8,128)(2,1)S(1)} %get-tuple-element.16), channel_id=1, replica_groups=mesh['task'=4,'param_0'=4,'param_1'=4,'param_2'=2] {'task'}, dimensions={0} | all-to-all | bytes 4194304 | tf_op jit(solution)/shard_map/all_to_all | solution.py:35
  34.9 3.6 %all-to-all-start.1 = ((bf16[4,2,128,1024]{3,2,1,0:T(8,128)(2,1)}), bf16[4,2,128,1024]{3,2,1,0:T(8,128)(2,1)S(1)}, u32[]{:S(2)}, u32[]{:S(2)}) async-start(bf16[4,2,128,1024]{3,2,1,0:T(8,128)(2,1)} %get-tuple-element.15), calls=%async_computation.1 | async-start | bytes 4194304 | tf_op jit(solution)/shard_map/all_to_all | solution.py:35
  44.1 3.1 %constant_dynamic-update-slice_fusion.1 = bf16[4,2,256,1024]{3,2,1,0:T(8,128)(2,1)} fusion(bf16[4,2,128,1024]{3,2,1,0:T(8,128)(2,1)} %all_to_all.10), kind=kLoop, calls=%fused_computation.5 | loop fusion | bytes 4194304
  47.3 15.7 %all-to-all-done.1 = bf16[4,2,128,1024]{3,2,1,0:T(8,128)(2,1)S(1)} async-done(((bf16[4,2,128,1024]{3,2,1,0:T(8,128)(2,1)}), bf16[4,2,128,1024]{3,2,1,0:T(8,128)(2,1)S(1)}, u32[]{:S(2)}, u32[]{:S(2)}) %all-to-all-start.1) | async-done | bytes 2097184 | tf_op jit(solution)/shard_map/all_to_all | solution.py:35
  62.9 1.6 constant_dynamic-update-slice_fusion
  64.6 4.5 %copy.5 = bf16[1,8,256,1024]{3,1,2,0:T(8,128)(2,1)S(1)} copy(bf16[1,8,256,1024]{3,2,1,0:T(8,128)(2,1)} %bitcast.32) | data formatting | bytes 8388608
  69.1 2.8 %fusion.11 = f32[8,8]{1,0:T(8,128)S(1)} fusion(bf16[8,262144]{1,0:T(8,128)(2,1)S(1)} %bitcast.31), kind=kOutput, calls=%fused_computation.66 | convolution fusion | flops 33554432 | bytes 4194560 | tf_op jit(solution)/shard_map/dot_general | solution.py:52
  71.9 6.9 %psum.56 = f32[8,8]{1,0:T(8,128)S(1)} all-reduce(f32[8,8]{1,0:T(8,128)S(1)} %fusion.11), channel_id=1, replica_groups=mesh['task'=4,'param_0'=4,'param_1'=4,'param_2'=2] {'task'}, use_global_device_ids=true, to_apply=%region_0.0 | all-reduce | flops 64 | bytes 512 | tf_op jit(solution)/shard_map/psum | solution.py:40
  78.7 9.7 %psum.57 = f32[8,8]{1,0:T(8,128)S(1)} all-reduce(f32[8,8]{1,0:T(8,128)S(1)} %psum.56), channel_id=1, replica_groups=mesh['task'=4,'param_0'=4,'param_1'=4,'param_2'=2] {'param_0'}, use_global_device_ids=true, to_apply=%region_1.0 | all-reduce | flops 64 | bytes 512 | tf_op jit(solution)/shard_map/psum | solution.py:40
  88.5 8.5 %psum.58 = f32[8,8]{1,0:T(8,128)S(1)} all-reduce(f32[8,8]{1,0:T(8,128)S(1)} %psum.57), channel_id=1, replica_groups=mesh['task'=4,'param_0'=4,'param_1'=4,'param_2'=2] {'param_1'}, use_global_device_ids=true, to_apply=%region_2.0 | all-reduce | flops 64 | bytes 512 | tf_op jit(solution)/shard_map/psum | solution.py:40
  96.9 11.0 %psum.59 = f32[8,8]{1,0:T(8,128)S(1)} all-reduce(f32[8,8]{1,0:T(8,128)S(1)} %psum.58), channel_id=1, replica_groups=mesh['task'=4,'param_0'=4,'param_1'=4,'param_2'=2] {'param_2'}, use_global_device_ids=true, to_apply=%region_3.0 | all-reduce | flops 64 | bytes 512 | tf_op jit(solution)/shard_map/psum | solution.py:40
  108.3 1.9 %fusion = (f32[]{:T(128)}, f32[]{:T(128)}) fusion(f32[8]{0:T(128)S(1)} %get-tuple-element.5, s32[]{:T(128)} %bitcast.1, f32[8]{0:T(128)S(1)} %get-tuple-element.12, s32[]{:T(128)} %bitcast.2), kind=kLoop, calls=%fused_computation.55 | loop fusion | flops 46 | bytes 80 | tf_op jit(solution)/shard_map/reduce_sum | solution.py:61
  113.1 1.8 %fusion.2 = (f32[]{:T(128)}, f32[]{:T(128)}) fusion(f32[8]{0:T(128)S(1)} %get-tuple-element.11, s32[]{:T(128)} %bitcast.3, f32[8]{0:T(128)S(1)} %get-tuple-element.10, s32[]{:T(128)} %bitcast.4), kind=kLoop, calls=%fused_computation.57 | loop fusion | flops 46 | bytes 80 | tf_op jit(solution)/shard_map/reduce_sum | solution.py:61
  115.5 0.7 divide_multiply_fusion.5
  117.8 1.8 %fusion.4 = (f32[]{:T(128)}, f32[]{:T(128)}) fusion(f32[8]{0:T(128)S(1)} %get-tuple-element.9, s32[]{:T(128)} %bitcast.5, f32[8]{0:T(128)S(1)} %get-tuple-element.8, s32[]{:T(128)} %bitcast.6), kind=kLoop, calls=%fused_computation.59 | loop fusion | flops 46 | bytes 80 | tf_op jit(solution)/shard_map/reduce_sum | solution.py:61
  122.5 1.8 %fusion.6 = (f32[]{:T(128)}, f32[]{:T(128)}) fusion(f32[8]{0:T(128)S(1)} %get-tuple-element.7, s32[]{:T(128)} %bitcast.7, f32[8]{0:T(128)S(1)} %get-tuple-element.6, s32[]{:T(128)} %bitcast.8), kind=kLoop, calls=%fused_computation.61 | loop fusion | flops 46 | bytes 80 | tf_op jit(solution)/shard_map/reduce_sum | solution.py:61
  127.7 8.7 %multiply_reduce_fusion = (f32[]{:T(128)}, f32[1,256,1024]{2,1,0:T(8,128)S(1)}) fusion(bf16[8,256,1024]{2,1,0:T(8,128)(2,1)} %bitcast.33, f32[]{:T(128)} %bitcast.17, f32[]{:T(128)} %bitcast.16, f32[]{:T(128)} %bitcast.15, f32[]{:T(128)} %bitcast.14, f32[]{:T(128)} %bitcast.13, f32[]{:T(128)} %bitcast.12, f32[]{:T(128)} %bitcast.11, f32[]{:T(128)} %bitcast.9), kind=kLoop, calls=%fused_computation.2 | loop fusion | flops 6553599 | bytes 5242916 | tf_op jit(solution)/shard_map/reduce_sum | solution.py:69
  136.4 7.2 %psum.60 = f32[]{:T(128)} all-reduce(f32[]{:T(128)} %get-tuple-element.13), channel_id=1, replica_groups=mesh['task'=4,'param_0'=4,'param_1'=4,'param_2'=2] {'task'}, use_global_device_ids=true, to_apply=%region_30.0 | all-reduce | flops 1 | bytes 8 | tf_op jit(solution)/shard_map/psum | solution.py:40
  143.6 6.6 %psum.61 = f32[]{:T(128)} all-reduce(f32[]{:T(128)} %psum.60), channel_id=1, replica_groups=mesh['task'=4,'param_0'=4,'param_1'=4,'param_2'=2] {'param_0'}, use_global_device_ids=true, to_apply=%region_31.0 | all-reduce | flops 1 | bytes 8 | tf_op jit(solution)/shard_map/psum | solution.py:40
  150.2 6.6 %psum.62 = f32[]{:T(128)} all-reduce(f32[]{:T(128)} %psum.61), channel_id=1, replica_groups=mesh['task'=4,'param_0'=4,'param_1'=4,'param_2'=2] {'param_1'}, use_global_device_ids=true, to_apply=%region_32.0 | all-reduce | flops 1 | bytes 8 | tf_op jit(solution)/shard_map/psum | solution.py:40
  156.8 8.6 %psum.63 = f32[]{:T(128)} all-reduce(f32[]{:T(128)} %psum.62), channel_id=1, replica_groups=mesh['task'=4,'param_0'=4,'param_1'=4,'param_2'=2] {'param_2'}, use_global_device_ids=true, to_apply=%region_33.0 | all-reduce | flops 1 | bytes 8 | tf_op jit(solution)/shard_map/psum | solution.py:40
  166.1 1.0 multiply_bitcast_fusion
  (29 shorter events, 12.3 us)
Async XLA Ops:
  4.4 34.1 %copy-start = (s32[8]{0:T(128)S(1)}, s32[8]{0:T(128)}, u32[]{:S(2)}) copy-start(s32[8]{0:T(128)} %param.3) | copy-start | bytes 100
  34.9 28.1 %all-to-all-start.1 = ((bf16[4,2,128,1024]{3,2,1,0:T(8,128)(2,1)}), bf16[4,2,128,1024]{3,2,1,0:T(8,128)(2,1)S(1)}, u32[]{:S(2)}, u32[]{:S(2)}) async-start(bf16[4,2,128,1024]{3,2,1,0:T(8,128)(2,1)} %get-tuple-element.15), calls=%async_computation.1 | async-start | bytes 4194304 | tf_op jit(solution)/shard_map/all_to_all | solution.py:35
where the time goes:
time: 168 us; the launch traced here: 167 us
  blocking collectives  95.5 us (57%)
  other arithmetic  28.7 us (17%)
  waiting for transfers between devices  15.7 us (9%)
  local copies, waits for them, and re-layouts  15 us (9%)
  between operations  5.92 us (4%)
  starting transfers between devices  3.61 us (2%)
  matrix products  2.79 us (2%)
    psum x8, blocking collectives, by_axis(): return functools.reduce(lax.psum, axes, value)  65 us
    all_to_all x1, blocking collectives, exchange_in_pieces(): lax.all_to_all(slab, axis, split_axis=0, concat_axis=0, tiled=True)  30.5 us
    all_to_all x1, waiting for transfers between devices, exchange_in_pieces(): lax.all_to_all(slab, axis, split_axis=0, concat_axis=0, tiled=True)  15.7 us
    reduce_sum x1, other arithmetic, shards(): energy = by_axis(jnp.sum(combined * combined), TASK_PARAM)  8.68 us
    unnamed x4, local copies, waits for them, and re-layouts  7.66 us
    reduce_sum x4, other arithmetic, shards(): norm_j = jnp.sum(column * picked)  7.34 us
    mul x8, other arithmetic, shards(): w = w * (1.0 - picked)  4.92 us
    convert_element_type x8, other arithmetic, shards(): picked = (labels == j).astype(jnp.float32)  4.9 us
  transfers between devices with their start and end apart: 1, of which 1 were waited for; matrix products, arithmetic and copies ran while one was open for 5% of the time, Pallas kernels for 0%

commit v1 on v0

v1 whole, which is shorter than its diff:
```python
import functools

import jax
import jax.numpy as jnp
from jax import lax
from jax.experimental import pallas as pl
from jax.experimental.pallas import tpu as pltpu
from jax.sharding import Mesh
from jax.sharding import PartitionSpec as P

PARAM = ("param_0", "param_1", "param_2")
TASK_PARAM = ("task", *PARAM)
CHUNKS = (64, 128, 64)
GRAIN = 16
OUT_ROWS = 64
LANES = 128
SUBLANES = 8
EPS = 1e-06
VMEM = pl.BlockSpec(memory_space=pltpu.VMEM)
SMEM = pl.BlockSpec(memory_space=pltpu.SMEM)


def places(order_ref, place_ref, tasks):
    for k in range(tasks):
        place_ref[order_ref[k]] = k


def slot_places(place_ref, me, parts, per):
    found = []
    for s in range(parts):
        first = lax.rem(me + (parts - s), parts) * per
        found += [place_ref[first + u] for u in range(per)]
    return found


def gram_kernel(parts, per, row0, first, last, order_ref, me_ref, own_ref, *refs):
    got, refs = refs[: parts - 1], refs[parts - 1 :]
    if not first:
        before_ref, refs = refs[0], refs[1:]
    out_ref, place_ref, *scratch = refs
    acc_ref = scratch[0] if last else out_ref
    tasks = parts * per
    rows, width = got[0].shape[1:]
    places(order_ref, place_ref, tasks)
    at = slot_places(place_ref, me_ref[0], parts, per)
    pairs = [(i, j) for i in range(tasks) for j in range(i, tasks)]

    def body(r, sums):
        sums = list(sums)
        for c in range(width // LANES):
            cols = pl.ds(c * LANES, LANES)
            x = [own_ref[u, pl.ds(row0 + r * GRAIN, GRAIN), cols] for u in range(per)]
            x += [g[u, pl.ds(r * GRAIN, GRAIN), cols] for g in got for u in range(per)]
            x = [v.astype(jnp.float32) for v in x]
            for h in range(GRAIN // SUBLANES):
                part = [v[h * SUBLANES : (h + 1) * SUBLANES] for v in x]
                for p, (i, j) in enumerate(pairs):
                    sums[p] = sums[p] + part[i] * part[j]
        return tuple(sums)

    zero = jnp.zeros((SUBLANES, LANES), jnp.float32)
    sums = lax.fori_loop(0, rows // GRAIN, body, (zero,) * len(pairs))
    square = tasks * tasks
    for p, (i, j) in enumerate(pairs):
        for a, b in ((i, j), (j, i))[: 1 if i == j else 2]:
            acc_ref[pl.ds(at[a] * tasks + at[b], SUBLANES, stride=square), :] = sums[p]
    if not first:
        acc_ref[...] += before_ref[...]
    if last:
        folded = acc_ref[:square, :]
        for k in range(1, SUBLANES):
            folded = folded + acc_ref[k * square : (k + 1) * square, :]
        folded = jnp.concatenate([folded, jnp.zeros((LANES - square, LANES), jnp.float32)], axis=0)
        row = lax.dot_general(
            jnp.ones((SUBLANES, LANES), jnp.float32), folded, (((1,), (1,)), ((), ())),
            precision=lax.Precision.HIGHEST, preferred_element_type=jnp.float32,
        )
        out_ref[...] = jnp.broadcast_to(row[:1], out_ref.shape)


def gram_of(order, me, own, got, before, row0, devices, last):
    per = own.shape[0]
    parts = len(got) + 1
    table = (SUBLANES * (parts * per) ** 2, LANES)
    first = before is None
    return pl.pallas_call(
        functools.partial(gram_kernel, parts, per, row0, first, last),
        in_specs=[SMEM, SMEM] + [VMEM] * (parts + (0 if first else 1)),
        out_specs=VMEM,
        out_shape=jax.ShapeDtypeStruct((devices, LANES) if last else table, jnp.float32),
        scratch_shapes=[pltpu.SMEM((parts * per,), jnp.int32)]
        + ([pltpu.VMEM(table, jnp.float32)] if last else []),
        compiler_params=pltpu.CompilerParams(vmem_limit_bytes=4 << 20),
        name="gram",
    )(order, me, own, *got, *([] if first else [before]))


def combine_kernel(parts, per, entries, order_ref, me_ref, gram_ref, own_ref, *refs):
    refs, (out_ref, place_ref, w_ref) = refs[:-3], refs[-3:]
    tasks = parts * per
    got = [refs[k : k + parts - 1] for k in range(0, len(refs), parts - 1)]
    step = pl.program_id(0)

    @pl.when(step == 0)
    def _():
        places(order_ref, place_ref, tasks)
        flat = jnp.sum(gram_ref[...], axis=0, keepdims=True)
        lane = lax.broadcasted_iota(jnp.int32, (tasks, LANES), 1)
        sub = lax.broadcasted_iota(jnp.int32, (tasks, LANES), 0)
        gram = jnp.concatenate(
            [pltpu.roll(flat, (LANES - tasks * k) % LANES, 1) for k in range(tasks)], axis=0
        )
        gram = jnp.where(lane < tasks, gram, 0.0)
        eye = lane == sub
        norm = jnp.sum(jnp.where(eye, gram, 0.0), axis=1, keepdims=True)
        inverse = jnp.broadcast_to(1.0 / (norm + EPS), (tasks, LANES))
        columns = [jnp.broadcast_to(gram[:, k : k + 1], (tasks, LANES)) for k in range(tasks)]
        coefs, dots = eye.astype(jnp.float32), gram
        for k in range(tasks):
            w = jnp.minimum(dots[k : k + 1, :], 0.0) * inverse[k : k + 1, :]
            w = jnp.broadcast_to(jnp.where(lane[:1] == k, 0.0, w), (tasks, LANES))
            coefs = coefs - jnp.where(sub == k, w, 0.0)
            dots = dots - columns[k] * w
        weight = jnp.sum(coefs, axis=1, keepdims=True)
        energy = jnp.sum(weight * jnp.sum(dots, axis=1, keepdims=True), axis=0, keepdims=True)
        rms = jnp.sqrt(jnp.maximum(energy, 0.0) / entries + EPS)
        w_ref[...] = jnp.broadcast_to(weight * (0.5 / rms), (tasks, LANES))

    at = slot_places(place_ref, me_ref[0], parts, per)
    weights = [jnp.broadcast_to(w_ref[pl.ds(a, 1), :], (GRAIN, LANES)) for a in at]
    width = out_ref.shape[1]
    row0 = 0
    for blocks in got:
        for top in range(0, blocks[0].shape[1], OUT_ROWS):

            @pl.when(step == (row0 + top) // OUT_ROWS)
            def _():
                for r in range(0, OUT_ROWS, GRAIN):
                    for c in range(0, width, LANES):
                        total = None
                        for s in range(parts):
                            for u in range(per):
                                if s == 0:
                                    x = own_ref[u, row0 + top + r : row0 + top + r + GRAIN, c : c + LANES]
                                else:
                                    x = blocks[s - 1][u, top + r : top + r + GRAIN, c : c + LANES]
                                term = weights[s * per + u] * x.astype(jnp.float32)
                                total = term if total is None else total + term
                        out_ref[r : r + GRAIN, c : c + LANES] = total

        row0 += blocks[0].shape[1]


def combine(order, me, gram, own, received, entries):
    per, rows, block = own.shape
    parts = len(received[0]) + 1
    flat = [b for got in received for b in got]
    return pl.pallas_call(
        functools.partial(combine_kernel, parts, per, entries),
        grid=(rows // OUT_ROWS,),
        in_specs=[SMEM, SMEM] + [VMEM] * (2 + len(flat)),
        out_specs=pl.BlockSpec((OUT_ROWS, block), lambda i: (i, 0)),
        out_shape=jax.ShapeDtypeStruct((rows, block), jnp.float32),
        scratch_shapes=[
            pltpu.SMEM((parts * per,), jnp.int32),
            pltpu.VMEM((parts * per, LANES), jnp.float32),
        ],
        compiler_params=pltpu.CompilerParams(vmem_limit_bytes=4 << 20),
        name="combine",
    )(order, me, gram, own, *flat)


def near(value):
    return pltpu.with_memory_space_constraint(value, pltpu.VMEM)


def shift(value, axis, by):
    n = lax.axis_size(axis)
    return near(lax.ppermute(value, axis, [(i, (i + by) % n) for i in range(n)]))


def shards(grads, order):
    per, rows, width = grads.shape
    parts, devices = lax.axis_size("task"), lax.axis_size(TASK_PARAM)
    block = width // parts
    entries = rows * lax.axis_size(PARAM) * width
    index = lax.axis_index("task")
    me = index.astype(jnp.int32).reshape(1)
    received, row0 = [], 0
    for size in CHUNKS:
        got = {}
        for s in (2, 1, 3):
            to = lax.rem(index + s, parts) * block
            got[s] = shift(lax.dynamic_slice(grads, (0, row0, to), (per, size, block)), "task", s)
        received.append([got[s] for s in (1, 2, 3)])
        row0 += size
    own = near(lax.dynamic_slice(grads, (0, 0, index * block), (per, rows, block)))
    gram, row0 = None, 0
    for size, got in zip(CHUNKS, received):
        gram = gram_of(order, me, own, got, gram, row0, devices, row0 + size == rows)
        row0 += size
    gram = lax.all_to_all(gram, TASK_PARAM, 0, 0, tiled=True)
    return combine(order, me, gram, own, received, entries)


def solution(mesh):
    torus = Mesh(
        mesh.devices.reshape(mesh.shape["task"], 4, 4, 2), ("task", "param_0", "param_1", "param_2")
    )
    in_specs = (P("task", PARAM, None), P())
    out_specs = P(PARAM, "task")
    return jax.shard_map(
        shards, mesh=torus, in_specs=in_specs, out_specs=out_specs, check_vma=False
    )
```

time: 168 us -> 79.6 us (0.47)
  blocking collectives: 95.5 us -> 18.8 us
  other arithmetic: 28.7 us -> 0 us
  waiting for transfers between devices: 15.7 us -> 35.5 us
  local copies, waits for them, and re-layouts: 15 us -> 6.08 us
  Pallas kernels: 0 us -> 8.25 us
  starting transfers between devices: 3.61 us -> 10.6 us
  between operations: 5.92 us -> 0.05 us
  matrix products: 2.79 us -> 0 us
    psum x8 -> x0, blocking collectives: 65 us -> none  [by_axis(): return functools.reduce(lax.psum, axes, value)]
    ppermute x0 -> x9, waiting for transfers between devices: none -> 35.5 us  [shift(): lax.ppermute(value, axis, [(i, (i + by) % n) for i in range(n)])]
    reduce_sum x15 -> x0, other arithmetic: 17.8 us -> none  [the longest x1 8.68 us: shards(): energy = by_axis(jnp.sum(combined * combined), TASK_PARAM)]
    all_to_all x1 -> x0, waiting for transfers between devices: 15.7 us -> none  [exchange_in_pieces(): lax.all_to_all(slab, axis, split_axis=0, concat_axis=0, tiled=True)]
    all_to_all x1, blocking collectives: 30.5 us -> 18.8 us  [shards(): gram = lax.all_to_all(gram, TASK_PARAM, 0, 0, tiled=True)]
    ppermute x0 -> x9, starting transfers between devices: none -> 10.6 us  [shift(): lax.ppermute(value, axis, [(i, (i + by) % n) for i in range(n)])]
    pallas_call x0 -> x4, Pallas kernels: none -> 8.25 us  [the longest x3 5.24 us: gram_of(): pl.pallas_call(functools.partial(gram_kernel, parts, per, row0, first, la...]
    unnamed x4 -> x2, local copies, waits for them, and re-layouts: 7.66 us -> 0.01 us
  transfers between devices with their start and end apart: 1 -> 9, of which waited for: 1 -> 6; matrix products, arithmetic and copies ran while one was open for 5% -> 5% of each run, Pallas kernels for 0% -> 5%
where the time goes in v1:
time: 79.6 us; the launch traced here: 79.4 us
  waiting for transfers between devices  35.5 us (45%)
  blocking collectives  18.8 us (24%)
  starting transfers between devices  10.6 us (13%)
  Pallas kernels  8.25 us (10%)
  local copies, waits for them, and re-layouts  6.08 us (8%)
    ppermute x9, waiting for transfers between devices, shift(): lax.ppermute(value, axis, [(i, (i + by) % n) for i in range(n)])  35.5 us
    all_to_all x1, blocking collectives, shards(): gram = lax.all_to_all(gram, TASK_PARAM, 0, 0, tiled=True)  18.8 us
    ppermute x9, starting transfers between devices, shift(): lax.ppermute(value, axis, [(i, (i + by) % n) for i in range(n)])  10.6 us
    pallas_call x3, Pallas kernels, gram_of(): pl.pallas_call(functools.partial(gram_kernel, parts, per, row0, first, la...  5.24 us
    dynamic_slice x2, local copies, waits for them, and re-layouts, shards(): lax.dynamic_slice(grads, (0, row0, to), (per, size, block))  4.79 us
    pallas_call x1, Pallas kernels, combine(): pl.pallas_call(functools.partial(combine_kernel, parts, per, entries), gr...  3.01 us
  transfers between devices with their start and end apart: 9, of which 6 were waited for; matrix products, arithmetic and copies ran while one was open for 5% of the time, Pallas kernels for 5%

profile of v1, /device:TPU:1, one launch (start us, length us, event | category | flops | bytes accessed | tf_op | source)
XLA Modules:
  0.0 79.4 jit_solution(4983957576701076061)
XLA Ops:
  0.0 2.3 %constant_dynamic-slice_fusion = (bf16[2,64,1024]{2,1,0:T(8,128)(2,1)S(1)}, bf16[2,64,1024]{2,1,0:T(8,128)(2,1)S(1)}, bf16[2,64,1024]{2,1,0:T(8,128)(2,1)}, bf16...) fusion(bf16[2,256,4096]{2,1,0:T(8,128)(2,1)} %param.2, s32[]{:T(128)S(6)} %select_n.21, ...), kind=kLoop, calls=%fused_computation | loop fusion | bytes 3145740 | tf_op jit(solution)/shard_map/dynamic_slice | solution.py:194
  2.3 3.6 %collective-permute-start.8 = (bf16[2,64,1024]{2,1,0:T(8,128)(2,1)S(1)}, bf16[2,64,1024]{2,1,0:T(8,128)(2,1)S(1)}, u32[]{:S(2)}, u32[]{:S(2)}) collective-permute-start(bf16[2,64,1024]{2,1,0:T(8,128)(2,1)S(1)} %get-tuple-element.5), channel_id=1, source_target_pairs={{0,96},{32,0},{64,32},{96,64},{1,97},{33,1},{65,33},{97,65},{2,98}... | collective-permute-start | bytes 786440 | tf_op jit(solution)/shard_map/ppermute | solution.py:179
  5.9 2.5 %constant_dynamic-slice_fusion.3 = (bf16[2,128,1024]{2,1,0:T(8,128)(2,1)S(1)}, bf16[2,128,1024]{2,1,0:T(8,128)(2,1)}, bf16[2,128,1024]{2,1,0:T(8,128)(2,1)}) fusion(bf16[2,256,4096]{2,1,0:T(8,128)(2,1)} %param.2, s32[]{:T(128)S(6)} %select_n.21, s32[]{:T(128)S(6)} %select_n.20, s32[]{:T(128)S(6)} %select_n.9), kind=kLoop, calls=%fused_computation.3 | loop fusion | bytes 3145740 | tf_op jit(solution)/shard_map/dynamic_slice | solution.py:194
  8.4 0.5 collective-permute-start.5
  8.8 1.0 %collective-permute-start.6 = (bf16[2,64,1024]{2,1,0:T(8,128)(2,1)S(1)}, bf16[2,64,1024]{2,1,0:T(8,128)(2,1)S(1)}, u32[]{:S(2)}, u32[]{:S(2)}) collective-permute-start(bf16[2,64,1024]{2,1,0:T(8,128)(2,1)S(1)} %get-tuple-element.6), channel_id=1, source_target_pairs={{0,32},{32,64},{64,96},{96,0},{1,33},{33,65},{65,97},{97,1},{2,34}... | collective-permute-start | bytes 786440 | tf_op jit(solution)/shard_map/ppermute | solution.py:179
  9.8 0.3 collective-permute-start.7
  10.2 2.6 %collective-permute-start.4 = (bf16[2,128,1024]{2,1,0:T(8,128)(2,1)}, bf16[2,128,1024]{2,1,0:T(8,128)(2,1)S(1)}, u32[]{:S(2)}, u32[]{:S(2)}) collective-permute-start(bf16[2,128,1024]{2,1,0:T(8,128)(2,1)} %get-tuple-element.12), channel_id=1, source_target_pairs={{0,64},{32,96},{64,0},{96,32},{1,65},{33,97},{65,1},{97,33},{2,66}... | collective-permute-start | bytes 1572872 | tf_op jit(solution)/shard_map/ppermute | solution.py:179
  12.8 0.0 collective-permute-done.8.refs_2_
  12.8 0.0 collective-permute-start.3
  12.8 5.1 %collective-permute-done.6.refs_0_ = bf16[2,64,1024]{2,1,0:T(8,128)(2,1)S(1)} collective-permute-done((bf16[2,64,1024]{2,1,0:T(8,128)(2,1)S(1)}, bf16[2,64,1024]{2,1,0:T(8,128)(2,1)S(1)}, u32[]{:S(2)}, u32[]{:S(2)}) %collective-permute-start.6) | collective-permute-done | bytes 262176 | tf_op jit(solution)/shard_map/ppermute | solution.py:179
  17.9 3.0 %collective-permute-done.7.refs_1_ = bf16[2,64,1024]{2,1,0:T(8,128)(2,1)S(1)} collective-permute-done((bf16[2,64,1024]{2,1,0:T(8,128)(2,1)S(1)}, bf16[2,64,1024]{2,1,0:T(8,128)(2,1)S(1)}, u32[]{:S(2)}, u32[]{:S(2)}) %collective-permute-start.7) | collective-permute-done | bytes 262176 | tf_op jit(solution)/shard_map/ppermute | solution.py:179
  20.9 2.6 %collective-permute-start.1 = (bf16[2,64,1024]{2,1,0:T(8,128)(2,1)}, bf16[2,64,1024]{2,1,0:T(8,128)(2,1)S(1)}, u32[]{:S(2)}, u32[]{:S(2)}) collective-permute-start(bf16[2,64,1024]{2,1,0:T(8,128)(2,1)} %get-tuple-element.8), channel_id=1, source_target_pairs={{0,64},{32,96},{64,0},{96,32},{1,65},{33,97},{65,1},{97,33},{2,66}... | collective-permute-start | bytes 786440 | tf_op jit(solution)/shard_map/ppermute | solution.py:179
  23.6 14.1 %collective-permute-done.5.refs_2_.refs_5_ = bf16[2,128,1024]{2,1,0:T(8,128)(2,1)S(1)} collective-permute-done((bf16[2,128,1024]{2,1,0:T(8,128)(2,1)S(1)}, bf16[2,128,1024]{2,1,0:T(8,128)(2,1)S(1)}, u32[]{:S(2)}, u32[]{:S(2)}) %collective-permute-start.5) | collective-permute-done | bytes 524320 | tf_op jit(solution)/shard_map/ppermute | solution.py:179
  37.7 0.0 collective-permute-start
  37.7 1.3 %constant_dynamic-slice_fusion.9.own_ref = bf16[2,256,1024]{2,1,0:T(8,128)(2,1)S(1)} fusion(bf16[2,256,4096]{2,1,0:T(8,128)(2,1)} %param.2, s32[]{:T(128)S(6)} %select_n.8), kind=kLoop, calls=%fused_computation.9 | loop fusion | bytes 2097156 | tf_op jit(solution)/shard_map/dynamic_slice | solution.py:197
  39.0 1.4 %gram.3.refs_3_ = f32[512,128]{1,0:T(8,128)S(1)} custom-call(s32[8]{0:T(128)S(1)} %copy-done, s32[1]{0:T(128)} %bitcast.me_ref, bf16[2,256,1024]{2,1,0:T(8,128)(2,1)S(1)} %constant_dynamic-slice_fusion.9.own_ref, bf16[2,64,1024]{2,1,0:T(8,128)(2,1)S(1)} %collective-permute-done.6.refs_0_, bf16[2,64,1024]{2,1,0:T(8,128)(2,1)S(1)} %collective-permute-done.7.refs_1_, ...), custom_call_target="tpu_custom_call" | custom-call | tf_op jit(solution)/shard_map/gram/pallas_call | solution.py:86
  40.5 0.0 collective-permute-done.4.refs_1_.refs_4_
  40.5 5.5 %collective-permute-done.3.refs_0_.refs_3_ = bf16[2,128,1024]{2,1,0:T(8,128)(2,1)S(1)} collective-permute-done((bf16[2,128,1024]{2,1,0:T(8,128)(2,1)}, bf16[2,128,1024]{2,1,0:T(8,128)(2,1)S(1)}, u32[]{:S(2)}, u32[]{:S(2)}) %collective-permute-start.3) | collective-permute-done | bytes 524320 | tf_op jit(solution)/shard_map/ppermute | solution.py:179
  46.0 2.2 %gram.4.refs_3_ = f32[512,128]{1,0:T(8,128)S(1)} custom-call(s32[8]{0:T(128)S(1)} %copy-done, s32[1]{0:T(128)} %bitcast.me_ref, bf16[2,256,1024]{2,1,0:T(8,128)(2,1)S(1)} %constant_dynamic-slice_fusion.9.own_ref, bf16[2,128,1024]{2,1,0:T(8,128)(2,1)S(1)} %collective-permute-done.3.refs_0_.refs_3_, ...), custom_call_target="tpu_custom_call" | custom-call | tf_op jit(solution)/shard_map/gram/pallas_call | solution.py:86
  48.2 2.0 %collective-permute-done.2.refs_2_.refs_8_ = bf16[2,64,1024]{2,1,0:T(8,128)(2,1)S(1)} collective-permute-done((bf16[2,64,1024]{2,1,0:T(8,128)(2,1)}, bf16[2,64,1024]{2,1,0:T(8,128)(2,1)S(1)}, u32[]{:S(2)}, u32[]{:S(2)}) %collective-permute-start.2) | collective-permute-done | bytes 262176 | tf_op jit(solution)/shard_map/ppermute | solution.py:179
  50.1 5.8 %collective-permute-done.refs_0_.refs_6_ = bf16[2,64,1024]{2,1,0:T(8,128)(2,1)S(1)} collective-permute-done((bf16[2,64,1024]{2,1,0:T(8,128)(2,1)S(1)}, bf16[2,64,1024]{2,1,0:T(8,128)(2,1)S(1)}, u32[]{:S(2)}, u32[]{:S(2)}) %collective-permute-start) | collective-permute-done | bytes 262176 | tf_op jit(solution)/shard_map/ppermute | solution.py:179
  55.9 1.6 %gram.5 = f32[128,128]{1,0:T(8,128)S(1)} custom-call(s32[8]{0:T(128)S(1)} %copy-done, s32[1]{0:T(128)} %bitcast.me_ref, bf16[2,256,1024]{2,1,0:T(8,128)(2,1)S(1)} %constant_dynamic-slice_fusion.9.own_ref, bf16[2,64,1024]{2,1,0:T(8,128)(2,1)S(1)} %collective-permute-done.refs_0_.refs_6_, bf16[2,64,1024]{2,1,0:T(8,128)(2,1)S(1)} %collective-permute-done.1.refs_1_.refs_7_, ...), custom_call_target="tpu_custom_call" | custom-call | tf_op jit(solution)/shard_map/gram/pallas_call | solution.py:86
  57.5 18.8 %all_to_all.11 = f32[128,1,128]{2,1,0:T(1,128)S(1)} all-to-all(f32[128,1,128]{2,1,0:T(1,128)S(1)} %bitcast.6), channel_id=1, replica_groups=mesh['task'=4,'param_0'=4,'param_1'=4,'param_2'=2] {'task','param_0','pa..., dimensions={0} | all-to-all | bytes 131072 | tf_op jit(solution)/shard_map/all_to_all | solution.py:202
  76.4 3.0 %combine.1 = f32[256,1024]{1,0:T(8,128)} custom-call(s32[8]{0:T(128)S(1)} %copy-done, s32[1]{0:T(128)} %bitcast.me_ref, f32[128,128]{1,0:T(8,128)S(1)} %bitcast.5, bf16[2,256,1024]{2,1,0:T(8,128)(2,1)S(1)} %constant_dynamic-slice_fusion.9.own_ref, bf16[2,64,1024]{2,1,0:T(8,128)(2,1)S(1)} %collective-permute-done.6.refs_0_, ...), custom_call_target="tpu_custom_call" | custom-call | tf_op jit(solution)/shard_map/combine/pallas_call | solution.py:158
  (4 shorter events, 0.0 us)
Async XLA Ops:
  0.0 39.0 %copy-start = (s32[8]{0:T(128)S(1)}, s32[8]{0:T(128)}, u32[]{:S(2)}) copy-start(s32[8]{0:T(128)} %order_ref.7) | copy-start | bytes 100
  2.3 10.5 %collective-permute-start.8 = (bf16[2,64,1024]{2,1,0:T(8,128)(2,1)S(1)}, bf16[2,64,1024]{2,1,0:T(8,128)(2,1)S(1)}, u32[]{:S(2)}, u32[]{:S(2)}) collective-permute-start(bf16[2,64,1024]{2,1,0:T(8,128)(2,1)S(1)} %get-tuple-element.5), channel_id=1, source_target_pairs={{0,96},{32,0},{64,32},{96,64},{1,97},{33,1},{65,33},{97,65},{2,98}... | collective-permute-start | bytes 786440 | tf_op jit(solution)/shard_map/ppermute | solution.py:179
  8.4 29.3 %collective-permute-start.5 = (bf16[2,128,1024]{2,1,0:T(8,128)(2,1)S(1)}, bf16[2,128,1024]{2,1,0:T(8,128)(2,1)S(1)}, u32[]{:S(2)}, u32[]{:S(2)}) collective-permute-start(bf16[2,128,1024]{2,1,0:T(8,128)(2,1)S(1)} %get-tuple-element.11), channel_id=1, source_target_pairs={{0,96},{32,0},{64,32},{96,64},{1,97},{33,1},{65,33},{97,65},{2,98}... | collective-permute-start | bytes 1572872 | tf_op jit(solution)/shard_map/ppermute | solution.py:179
  8.8 9.1 %collective-permute-start.6 = (bf16[2,64,1024]{2,1,0:T(8,128)(2,1)S(1)}, bf16[2,64,1024]{2,1,0:T(8,128)(2,1)S(1)}, u32[]{:S(2)}, u32[]{:S(2)}) collective-permute-start(bf16[2,64,1024]{2,1,0:T(8,128)(2,1)S(1)} %get-tuple-element.6), channel_id=1, source_target_pairs={{0,32},{32,64},{64,96},{96,0},{1,33},{33,65},{65,97},{97,1},{2,34}... | collective-permute-start | bytes 786440 | tf_op jit(solution)/shard_map/ppermute | solution.py:179
  9.8 11.1 %collective-permute-start.7 = (bf16[2,64,1024]{2,1,0:T(8,128)(2,1)S(1)}, bf16[2,64,1024]{2,1,0:T(8,128)(2,1)S(1)}, u32[]{:S(2)}, u32[]{:S(2)}) collective-permute-start(bf16[2,64,1024]{2,1,0:T(8,128)(2,1)S(1)} %get-tuple-element.10), channel_id=1, source_target_pairs={{0,64},{32,96},{64,0},{96,32},{1,65},{33,97},{65,1},{97,33},{2,66}... | collective-permute-start | bytes 786440 | tf_op jit(solution)/shard_map/ppermute | solution.py:179
  10.2 30.3 %collective-permute-start.4 = (bf16[2,128,1024]{2,1,0:T(8,128)(2,1)}, bf16[2,128,1024]{2,1,0:T(8,128)(2,1)S(1)}, u32[]{:S(2)}, u32[]{:S(2)}) collective-permute-start(bf16[2,128,1024]{2,1,0:T(8,128)(2,1)} %get-tuple-element.12), channel_id=1, source_target_pairs={{0,64},{32,96},{64,0},{96,32},{1,65},{33,97},{65,1},{97,33},{2,66}... | collective-permute-start | bytes 1572872 | tf_op jit(solution)/shard_map/ppermute | solution.py:179
  12.8 33.2 %collective-permute-start.3 = (bf16[2,128,1024]{2,1,0:T(8,128)(2,1)}, bf16[2,128,1024]{2,1,0:T(8,128)(2,1)S(1)}, u32[]{:S(2)}, u32[]{:S(2)}) collective-permute-start(bf16[2,128,1024]{2,1,0:T(8,128)(2,1)} %get-tuple-element.13), channel_id=1, source_target_pairs={{0,32},{32,64},{64,96},{96,0},{1,33},{33,65},{65,97},{97,1},{2,34}... | collective-permute-start | bytes 1572872 | tf_op jit(solution)/shard_map/ppermute | solution.py:179
  17.9 32.2 %collective-permute-start.2 = (bf16[2,64,1024]{2,1,0:T(8,128)(2,1)}, bf16[2,64,1024]{2,1,0:T(8,128)(2,1)S(1)}, u32[]{:S(2)}, u32[]{:S(2)}) collective-permute-start(bf16[2,64,1024]{2,1,0:T(8,128)(2,1)} %get-tuple-element.7), channel_id=1, source_target_pairs={{0,96},{32,0},{64,32},{96,64},{1,97},{33,1},{65,33},{97,65},{2,98}... | collective-permute-start | bytes 786440 | tf_op jit(solution)/shard_map/ppermute | solution.py:179
  20.9 29.2 %collective-permute-start.1 = (bf16[2,64,1024]{2,1,0:T(8,128)(2,1)}, bf16[2,64,1024]{2,1,0:T(8,128)(2,1)S(1)}, u32[]{:S(2)}, u32[]{:S(2)}) collective-permute-start(bf16[2,64,1024]{2,1,0:T(8,128)(2,1)} %get-tuple-element.8), channel_id=1, source_target_pairs={{0,64},{32,96},{64,0},{96,32},{1,65},{33,97},{65,1},{97,33},{2,66}... | collective-permute-start | bytes 786440 | tf_op jit(solution)/shard_map/ppermute | solution.py:179
  37.7 18.2 %collective-permute-start = (bf16[2,64,1024]{2,1,0:T(8,128)(2,1)S(1)}, bf16[2,64,1024]{2,1,0:T(8,128)(2,1)S(1)}, u32[]{:S(2)}, u32[]{:S(2)}) collective-permute-start(bf16[2,64,1024]{2,1,0:T(8,128)(2,1)S(1)} %get-tuple-element.9), channel_id=1, source_target_pairs={{0,32},{32,64},{64,96},{96,0},{1,33},{33,65},{65,97},{97,1},{2,34}... | collective-permute-start | bytes 786440 | tf_op jit(solution)/shard_map/ppermute | solution.py:179

commit v2 on v1

v2 whole, which is shorter than its diff:
```python
import functools

import jax
import jax.numpy as jnp
from jax import lax
from jax.experimental import pallas as pl
from jax.experimental.pallas import tpu as pltpu
from jax.sharding import Mesh
from jax.sharding import PartitionSpec as P

PARAM = ("param_0", "param_1", "param_2")
TASK_PARAM = ("task", *PARAM)
CHUNKS = (192, 64)
GRAIN = 16
OUT_ROWS = 64
LANES = 128
SUBLANES = 8
EPS = 1e-06
VMEM = pl.BlockSpec(memory_space=pltpu.VMEM)
SMEM = pl.BlockSpec(memory_space=pltpu.SMEM)


def slot_tasks(parts, per):
    me = lax.axis_index("task")
    return [lax.rem(me + (parts - s), parts) * per + u for s in range(parts) for u in range(per)]


def tables(order_ref, slots, select_ref, pick_ref):
    tasks = len(slots)
    left = lax.broadcasted_iota(jnp.int32, (LANES, LANES), 0)
    right = lax.broadcasted_iota(jnp.int32, (LANES, LANES), 1)
    first, second = jnp.full((LANES, LANES), -1, jnp.int32), jnp.zeros((LANES, LANES), jnp.int32)
    place = lax.broadcasted_iota(jnp.int32, (tasks, LANES), 0)
    ordered = jnp.zeros((tasks, LANES), jnp.int32)
    for k in range(tasks):
        first = jnp.where(right // tasks == k, order_ref[k], first)
        second = jnp.where(right % tasks == k, order_ref[k], second)
        ordered = jnp.where(place == k, order_ref[k], ordered)
    meet = (first >= 0) & (left == first * tasks + second)
    select_ref[...] = jnp.where(meet, 1.0, 0.0)
    for i, task in enumerate(slots):
        pick_ref[i] = jnp.where(ordered == task, 1.0, 0.0)


def gram_kernel(parts, per, row0, first, last, *refs):
    if first:
        order_ref, refs = refs[0], refs[1:]
    own_ref, got, refs = refs[0], refs[1:parts], refs[parts:]
    if not first:
        before_ref, refs = refs[0], refs[1:]
    out_ref, *refs = refs
    acc_ref = refs[-1] if last else out_ref
    tasks = parts * per
    rows, width = got[0].shape[1:]
    slots = slot_tasks(parts, per)
    pairs = [(i, j) for i in range(tasks) for j in range(i, tasks)]

    def body(r, sums):
        sums = list(sums)
        for c in range(width // LANES):
            cols = pl.ds(c * LANES, LANES)
            x = [own_ref[u, pl.ds(row0 + r * GRAIN, GRAIN), cols] for u in range(per)]
            x += [g[u, pl.ds(r * GRAIN, GRAIN), cols] for g in got for u in range(per)]
            x = [v.astype(jnp.float32) for v in x]
            for h in range(GRAIN // SUBLANES):
                part = [v[h * SUBLANES : (h + 1) * SUBLANES] for v in x]
                for p, (i, j) in enumerate(pairs):
                    sums[p] = sums[p] + part[i] * part[j]
        return tuple(sums)

    zero = jnp.zeros((SUBLANES, LANES), jnp.float32)
    sums = lax.fori_loop(0, rows // GRAIN, body, (zero,) * len(pairs))
    square = tasks * tasks
    for p, (i, j) in enumerate(pairs):
        for a, b in ((i, j), (j, i))[: 1 if i == j else 2]:
            acc_ref[pl.ds(slots[a] * tasks + slots[b], SUBLANES, stride=square), :] = sums[p]
    if not first:
        acc_ref[...] += before_ref[...]
    if first:
        tables(order_ref, slots, *refs[:2])
    if last:
        folded = acc_ref[:square, :]
        for k in range(1, SUBLANES):
            folded = folded + acc_ref[k * square : (k + 1) * square, :]
        folded = jnp.concatenate([folded, jnp.zeros((LANES - square, LANES), jnp.float32)], axis=0)
        row = lax.dot_general(
            jnp.ones((SUBLANES, LANES), jnp.float32), folded, (((1,), (1,)), ((), ())),
            precision=lax.Precision.HIGHEST, preferred_element_type=jnp.float32,
        )
        out_ref[...] = jnp.broadcast_to(row[:1], out_ref.shape)


def gram_of(order, own, got, before, row0, devices, last):
    per = own.shape[0]
    parts = len(got) + 1
    tasks = parts * per
    table = (SUBLANES * tasks**2, LANES)
    first = before is None
    shapes = [(devices, LANES) if last else table]
    if first:
        shapes += [(LANES, LANES), (tasks, tasks, LANES)]
    return pl.pallas_call(
        functools.partial(gram_kernel, parts, per, row0, first, last),
        in_specs=[SMEM] * first + [VMEM] * (parts + (not first)),
        out_specs=[VMEM] * len(shapes),
        out_shape=[jax.ShapeDtypeStruct(shape, jnp.float32) for shape in shapes],
        scratch_shapes=[pltpu.VMEM(table, jnp.float32)] if last else [],
        compiler_params=pltpu.CompilerParams(vmem_limit_bytes=4 << 20),
        name="gram",
    )(*([order] if first else []), own, *got, *([] if first else [before]))


def combine_kernel(parts, per, entries, gram_ref, select_ref, pick_ref, own_ref, *refs):
    refs, (out_ref, rows_ref, sems) = refs[:-3], refs[-3:]
    tasks = parts * per
    got = [refs[k : k + parts - 1] for k in range(0, len(refs), parts - 1)]
    flat = jnp.sum(gram_ref[...], axis=0, keepdims=True)
    flat = lax.dot_general(
        jnp.broadcast_to(flat, (SUBLANES, LANES)), select_ref[...], (((1,), (0,)), ((), ())),
        precision=lax.Precision.HIGHEST, preferred_element_type=jnp.float32,
    )[:1]
    lane = lax.broadcasted_iota(jnp.int32, (tasks, LANES), 1)
    sub = lax.broadcasted_iota(jnp.int32, (tasks, LANES), 0)
    gram = jnp.concatenate(
        [pltpu.roll(flat, (LANES - tasks * k) % LANES, 1) for k in range(tasks)], axis=0
    )
    gram = jnp.where(lane < tasks, gram, 0.0)
    eye = lane == sub
    norm = jnp.sum(jnp.where(eye, gram, 0.0), axis=1, keepdims=True)
    inverse = jnp.broadcast_to(1.0 / (norm + EPS), (tasks, LANES))
    columns = [jnp.broadcast_to(gram[:, k : k + 1], (tasks, LANES)) for k in range(tasks)]
    coefs, dots = eye.astype(jnp.float32), gram
    for k in range(tasks):
        w = jnp.minimum(dots[k : k + 1, :], 0.0) * inverse[k : k + 1, :]
        w = jnp.broadcast_to(jnp.where(lane[:1] == k, 0.0, w), (tasks, LANES))
        coefs = coefs - jnp.where(sub == k, w, 0.0)
        dots = dots - columns[k] * w
    weight = jnp.sum(coefs, axis=1, keepdims=True)
    energy = jnp.sum(weight * jnp.sum(dots, axis=1, keepdims=True), axis=0, keepdims=True)
    rms = jnp.sqrt(jnp.maximum(energy, 0.0) / entries + EPS)
    weight = jnp.broadcast_to(weight * (0.5 / rms), (tasks, LANES))
    weights = [
        jnp.broadcast_to(jnp.sum(pick_ref[i] * weight, axis=0, keepdims=True), (GRAIN, LANES))
        for i in range(tasks)
    ]
    width = rows_ref.shape[1]
    copies, row0 = [], 0
    for blocks in got:
        size = blocks[0].shape[1]
        for top in range(0, size, OUT_ROWS):
            here = min(OUT_ROWS, size - top)

            def body(r, _):
                at = pl.multiple_of(top + r * GRAIN, GRAIN)
                for c in range(0, width, LANES):
                    cols = pl.ds(c, LANES)
                    total = None
                    for s in range(parts):
                        for u in range(per):
                            if s == 0:
                                x = own_ref[u, pl.ds(row0 + at, GRAIN), cols]
                            else:
                                x = blocks[s - 1][u, pl.ds(at, GRAIN), cols]
                            term = weights[s * per + u] * x.astype(jnp.float32)
                            total = term if total is None else total + term
                    rows_ref[pl.ds(row0 + at, GRAIN), cols] = total
                return 0

            lax.fori_loop(0, here // GRAIN, body, 0)
            span = pl.ds(row0 + top, here)
            copy = pltpu.make_async_copy(rows_ref.at[span], out_ref.at[span], sems.at[len(copies)])
            copy.start()
            copies.append(copy)
        row0 += size
    for copy in copies:
        copy.wait()


def combine(gram, select, pick, own, received, entries):
    per, rows, block = own.shape
    parts = len(received[0]) + 1
    flat = [b for got in received for b in got]
    pieces = sum(-(-got[0].shape[1] // OUT_ROWS) for got in received)
    return pl.pallas_call(
        functools.partial(combine_kernel, parts, per, entries),
        in_specs=[VMEM] * (4 + len(flat)),
        out_specs=pl.BlockSpec(memory_space=pltpu.HBM),
        out_shape=jax.ShapeDtypeStruct((rows, block), jnp.float32),
        scratch_shapes=[
            pltpu.VMEM((rows, block), jnp.float32),
            pltpu.SemaphoreType.DMA((pieces,)),
        ],
        compiler_params=pltpu.CompilerParams(vmem_limit_bytes=4 << 20),
        name="combine",
    )(gram, select, pick, own, *flat)


def cut_kernel(parts, shifts, spans, grads_ref, *refs):
    outs, sems = refs[:-1], refs[-1]
    block = outs[0].shape[-1]
    me = lax.axis_index("task")
    copies = []
    for row0, size in spans:
        for s in shifts:
            column = pl.multiple_of(lax.rem(me + s, parts) * block, block)
            source = grads_ref.at[:, pl.ds(row0, size), pl.ds(column, block)]
            k = len(copies)
            copies.append(pltpu.make_async_copy(source, outs[k], sems.at[k]))
    for copy in copies:
        copy.start()
    for copy in copies:
        copy.wait()


def cut(grads, parts, shifts, spans):
    per, _, width = grads.shape
    shapes = [(per, size, width // parts) for _, size in spans for _ in shifts]
    cuts = pl.pallas_call(
        functools.partial(cut_kernel, parts, shifts, spans),
        in_specs=[pl.BlockSpec(memory_space=pltpu.HBM)],
        out_specs=[VMEM] * len(shapes),
        out_shape=[pltpu.VMEM(shape, grads.dtype) for shape in shapes],
        scratch_shapes=[pltpu.SemaphoreType.DMA((len(shapes),))],
        compiler_params=pltpu.CompilerParams(vmem_limit_bytes=4 << 20),
        name="cut",
    )(pltpu.with_memory_space_constraint(grads, pltpu.HBM))
    return [near(c) for c in cuts]


def near(value):
    return pltpu.with_memory_space_constraint(value, pltpu.VMEM)


def shift(value, axis, by):
    n = lax.axis_size(axis)
    return near(lax.ppermute(value, axis, [(i, (i + by) % n) for i in range(n)]))


def shards(grads, order):
    per, rows, width = grads.shape
    parts, devices = lax.axis_size("task"), lax.axis_size(TASK_PARAM)
    entries = rows * lax.axis_size(PARAM) * width
    shifts, received, row0 = (2, 1, 3), [], 0
    for size in CHUNKS:
        cuts = cut(grads, parts, shifts, [(row0, size)])
        got = {s: shift(c, "task", s) for s, c in zip(shifts, cuts)}
        received.append([got[s] for s in range(1, parts)])
        row0 += size
    own = cut(grads, parts, (0,), [(0, rows)])[0]
    gram, row0 = None, 0
    for size, got in zip(CHUNKS, received):
        gram, *more = gram_of(order, own, got, gram, row0, devices, row0 + size == rows)
        if more:
            select, pick = more
        row0 += size
    gram = lax.all_to_all(gram, TASK_PARAM, 0, 0, tiled=True)
    return combine(gram, select, pick, own, received, entries)


def solution(mesh):
    torus = Mesh(
        mesh.devices.reshape(mesh.shape["task"], 4, 4, 2), ("task", "param_0", "param_1", "param_2")
    )
    in_specs = (P("task", PARAM, None), P())
    out_specs = P(PARAM, "task")
    return jax.shard_map(
        shards, mesh=torus, in_specs=in_specs, out_specs=out_specs, check_vma=False
    )
```

time: 79.6 us -> 75.2 us (0.945)
  local copies, waits for them, and re-layouts: 6.08 us -> 0.01 us
  starting transfers between devices: 10.6 us -> 8.44 us
  Pallas kernels: 8.25 us -> 10.1 us
  blocking collectives: 18.8 us -> 20.2 us
    dynamic_slice x3 -> x0, local copies, waits for them, and re-layouts: 6.08 us -> none  [the longest x2 4.79 us: shards(): lax.dynamic_slice(grads, (0, row0, to), (per, size, block))]
    pallas_call x1 -> x4, Pallas kernels: 3.01 us -> 6.15 us  [the longest x3 4.01 us: cut(): pl.pallas_call(functools.partial(cut_kernel, parts, shifts, spans), in_sp...]
    ppermute x9 -> x6, starting transfers between devices: 10.6 us -> 8.44 us  [shift(): lax.ppermute(value, axis, [(i, (i + by) % n) for i in range(n)])]
    all_to_all x1, blocking collectives: 18.8 us -> 20.2 us  [shards(): gram = lax.all_to_all(gram, TASK_PARAM, 0, 0, tiled=True)]
    pallas_call x3 -> x2, Pallas kernels: 5.24 us -> 3.94 us  [gram_of(): pl.pallas_call(functools.partial(gram_kernel, parts, per, row0, first, la...]
    ppermute x9 -> x6, waiting for transfers between devices: 35.5 us -> 36.2 us  [shift(): lax.ppermute(value, axis, [(i, (i + by) % n) for i in range(n)])]
  transfers between devices with their start and end apart: 9 -> 6, of which waited for: 6 -> 4; matrix products, arithmetic and copies ran while one was open for 5% -> 0% of each run, Pallas kernels for 5% -> 7%
where the time goes in v2:
time: 75.2 us; the launch traced here: 75 us
  waiting for transfers between devices  36.2 us (48%)
  blocking collectives  20.2 us (27%)
  Pallas kernels  10.1 us (13%)
  starting transfers between devices  8.44 us (11%)
    ppermute x6, waiting for transfers between devices, shift(): lax.ppermute(value, axis, [(i, (i + by) % n) for i in range(n)])  36.2 us
    all_to_all x1, blocking collectives, shards(): gram = lax.all_to_all(gram, TASK_PARAM, 0, 0, tiled=True)  20.2 us
    ppermute x6, starting transfers between devices, shift(): lax.ppermute(value, axis, [(i, (i + by) % n) for i in range(n)])  8.44 us
    pallas_call x3, Pallas kernels, cut(): pl.pallas_call(functools.partial(cut_kernel, parts, shifts, spans), in_sp...  4.01 us
    pallas_call x2, Pallas kernels, gram_of(): pl.pallas_call(functools.partial(gram_kernel, parts, per, row0, first, la...  3.94 us
    pallas_call x1, Pallas kernels, combine(): pl.pallas_call(functools.partial(combine_kernel, parts, per, entries), in...  2.14 us
  transfers between devices with their start and end apart: 6, of which 4 were waited for; matrix products, arithmetic and copies ran while one was open for 0% of the time, Pallas kernels for 7%

profile of v2, /device:TPU:1, one launch (start us, length us, event | category | flops | bytes accessed | tf_op | source)
XLA Modules:
  0.0 75.0 jit_solution(15968405415693773258)
XLA Ops:
  0.0 1.6 %cut.5 = (bf16[2,192,1024]{2,1,0:T(8,128)(2,1)S(1)}, bf16[2,192,1024]{2,1,0:T(8,128)(2,1)S(1)}, bf16[2,192,1024]{2,1,0:T(8,128)(2,1)S(1)}) custom-call(bf16[2,256,4096]{2,1,0:T(8,128)(2,1)} %grads_ref.5), custom_call_target="tpu_custom_call" | custom-call | tf_op jit(solution)/shard_map/cut/pallas_call | solution.py:218
  1.7 2.2 %collective-permute-start.3 = (bf16[2,192,1024]{2,1,0:T(8,128)(2,1)S(1)}, bf16[2,192,1024]{2,1,0:T(8,128)(2,1)S(1)}, u32[]{:S(2)}, u32[]{:S(2)}) collective-permute-start(bf16[2,192,1024]{2,1,0:T(8,128)(2,1)S(1)} %get-tuple-element.17), channel_id=1, source_target_pairs={{0,32},{32,64},{64,96},{96,0},{1,33},{33,65},{65,97},{97,1},{2,34}... | collective-permute-start | bytes 2359304 | tf_op jit(solution)/shard_map/ppermute | solution.py:236
  3.8 2.6 %collective-permute-start.4 = (bf16[2,192,1024]{2,1,0:T(8,128)(2,1)S(1)}, bf16[2,192,1024]{2,1,0:T(8,128)(2,1)S(1)}, u32[]{:S(2)}, u32[]{:S(2)}) collective-permute-start(bf16[2,192,1024]{2,1,0:T(8,128)(2,1)S(1)} %get-tuple-element.18), channel_id=1, source_target_pairs={{0,64},{32,96},{64,0},{96,32},{1,65},{33,97},{65,1},{97,33},{2,66}... | collective-permute-start | bytes 2359304 | tf_op jit(solution)/shard_map/ppermute | solution.py:236
  6.5 0.0 copy-start
  6.5 1.1 %collective-permute-start.5 = (bf16[2,192,1024]{2,1,0:T(8,128)(2,1)S(1)}, bf16[2,192,1024]{2,1,0:T(8,128)(2,1)S(1)}, u32[]{:S(2)}, u32[]{:S(2)}) collective-permute-start(bf16[2,192,1024]{2,1,0:T(8,128)(2,1)S(1)} %get-tuple-element.19), channel_id=1, source_target_pairs={{0,96},{32,0},{64,32},{96,64},{1,97},{33,1},{65,33},{97,65},{2,98}... | collective-permute-start | bytes 2359304 | tf_op jit(solution)/shard_map/ppermute | solution.py:236
  7.5 1.1 %cut.4 = (bf16[2,64,1024]{2,1,0:T(8,128)(2,1)S(1)}, bf16[2,64,1024]{2,1,0:T(8,128)(2,1)S(1)}, bf16[2,64,1024]{2,1,0:T(8,128)(2,1)S(1)}) custom-call(bf16[2,256,4096]{2,1,0:T(8,128)(2,1)} %grads_ref.5), custom_call_target="tpu_custom_call" | custom-call | tf_op jit(solution)/shard_map/cut/pallas_call | solution.py:218
  8.7 0.5 collective-permute-start
  9.2 0.8 %collective-permute-start.1 = (bf16[2,64,1024]{2,1,0:T(8,128)(2,1)S(1)}, bf16[2,64,1024]{2,1,0:T(8,128)(2,1)S(1)}, u32[]{:S(2)}, u32[]{:S(2)}) collective-permute-start(bf16[2,64,1024]{2,1,0:T(8,128)(2,1)S(1)} %get-tuple-element.15), channel_id=1, source_target_pairs={{0,64},{32,96},{64,0},{96,32},{1,65},{33,97},{65,1},{97,33},{2,66}... | collective-permute-start | bytes 786440 | tf_op jit(solution)/shard_map/ppermute | solution.py:236
  9.9 12.4 %collective-permute-done.3.refs_2_.refs_0_ = bf16[2,192,1024]{2,1,0:T(8,128)(2,1)S(1)} collective-permute-done((bf16[2,192,1024]{2,1,0:T(8,128)(2,1)S(1)}, bf16[2,192,1024]{2,1,0:T(8,128)(2,1)S(1)}, u32[]{:S(2)}, u32[]{:S(2)}) %collective-permute-start.3) | collective-permute-done | bytes 786464 | tf_op jit(solution)/shard_map/ppermute | solution.py:236
  22.4 1.3 %collective-permute-start.2 = (bf16[2,64,1024]{2,1,0:T(8,128)(2,1)S(1)}, bf16[2,64,1024]{2,1,0:T(8,128)(2,1)S(1)}, u32[]{:S(2)}, u32[]{:S(2)}) collective-permute-start(bf16[2,64,1024]{2,1,0:T(8,128)(2,1)S(1)} %get-tuple-element.16), channel_id=1, source_target_pairs={{0,96},{32,0},{64,32},{96,64},{1,97},{33,1},{65,33},{97,65},{2,98}... | collective-permute-start | bytes 786440 | tf_op jit(solution)/shard_map/ppermute | solution.py:236
  23.7 1.2 %cut.3.refs_1_.refs_0_.own_ref = bf16[2,256,1024]{2,1,0:T(8,128)(2,1)S(1)} custom-call(bf16[2,256,4096]{2,1,0:T(8,128)(2,1)} %grads_ref.5), custom_call_target="tpu_custom_call" | custom-call | tf_op jit(solution)/shard_map/cut/pallas_call | solution.py:218
  24.9 15.4 %collective-permute-done.4.refs_3_.refs_1_ = bf16[2,192,1024]{2,1,0:T(8,128)(2,1)S(1)} collective-permute-done((bf16[2,192,1024]{2,1,0:T(8,128)(2,1)S(1)}, bf16[2,192,1024]{2,1,0:T(8,128)(2,1)S(1)}, u32[]{:S(2)}, u32[]{:S(2)}) %collective-permute-start.4) | collective-permute-done | bytes 786464 | tf_op jit(solution)/shard_map/ppermute | solution.py:236
  40.3 0.0 collective-permute-done.5.refs_4_.refs_2_
  40.4 0.0 copy-done
  40.4 2.9 %gram.2 = (f32[512,128]{1,0:T(8,128)S(1)}, f32[128,128]{1,0:T(8,128)S(1)}, f32[8,8,128]{2,1,0:T(8,128)S(1)}) custom-call(s32[8]{0:T(128)S(1)} %copy-done, bf16[2,256,1024]{2,1,0:T(8,128)(2,1)S(1)} %cut.3.refs_1_.refs_0_.own_ref, bf16[2,192,1024]{2,1,0:T(8,128)(2,1)S(1)} %collective-permute-done.3.refs_2_.refs_0_, ...), custom_call_target="tpu_custom_call" | custom-call | tf_op jit(solution)/shard_map/gram/pallas_call | solution.py:102
  43.3 1.6 %collective-permute-done.refs_1_.refs_3_ = bf16[2,64,1024]{2,1,0:T(8,128)(2,1)S(1)} collective-permute-done((bf16[2,64,1024]{2,1,0:T(8,128)(2,1)S(1)}, bf16[2,64,1024]{2,1,0:T(8,128)(2,1)S(1)}, u32[]{:S(2)}, u32[]{:S(2)}) %collective-permute-start) | collective-permute-done | bytes 262176 | tf_op jit(solution)/shard_map/ppermute | solution.py:236
  44.9 6.7 %collective-permute-done.1.refs_2_.refs_4_ = bf16[2,64,1024]{2,1,0:T(8,128)(2,1)S(1)} collective-permute-done((bf16[2,64,1024]{2,1,0:T(8,128)(2,1)S(1)}, bf16[2,64,1024]{2,1,0:T(8,128)(2,1)S(1)}, u32[]{:S(2)}, u32[]{:S(2)}) %collective-permute-start.1) | collective-permute-done | bytes 262176 | tf_op jit(solution)/shard_map/ppermute | solution.py:236
  51.5 0.0 collective-permute-done.2.refs_3_.refs_5_
  51.5 1.0 %gram.3 = f32[128,128]{1,0:T(8,128)S(1)} custom-call(bf16[2,256,1024]{2,1,0:T(8,128)(2,1)S(1)} %cut.3.refs_1_.refs_0_.own_ref, bf16[2,64,1024]{2,1,0:T(8,128)(2,1)S(1)} %collective-permute-done.refs_1_.refs_3_, bf16[2,64,1024]{2,1,0:T(8,128)(2,1)S(1)} %collective-permute-done.1.refs_2_.refs_4_, ...), custom_call_target="tpu_custom_call" | custom-call | tf_op jit(solution)/shard_map/gram/pallas_call | solution.py:102
  52.6 20.2 %all_to_all.11 = f32[128,1,128]{2,1,0:T(1,128)S(1)} all-to-all(f32[128,1,128]{2,1,0:T(1,128)S(1)} %bitcast.5), channel_id=1, replica_groups=mesh['task'=4,'param_0'=4,'param_1'=4,'param_2'=2] {'task','param_0','pa..., dimensions={0} | all-to-all | bytes 131072 | tf_op jit(solution)/shard_map/all_to_all | solution.py:256
  72.8 2.1 %combine.1 = f32[256,1024]{1,0:T(8,128)} custom-call(f32[128,128]{1,0:T(8,128)S(1)} %bitcast.4, f32[128,128]{1,0:T(8,128)S(1)} %get-tuple-element.21.select_ref, f32[8,8,128]{2,1,0:T(8,128)S(1)} %get-tuple-element.22.pick_ref, bf16[2,256,1024]{2,1,0:T(8,128)(2,1)S(1)} %cut.3.refs_1_.refs_0_.own_ref, ...), custom_call_target="tpu_custom_call" | custom-call | tf_op jit(solution)/shard_map/combine/pallas_call | solution.py:184
Async XLA Ops:
  1.7 20.7 %collective-permute-start.3 = (bf16[2,192,1024]{2,1,0:T(8,128)(2,1)S(1)}, bf16[2,192,1024]{2,1,0:T(8,128)(2,1)S(1)}, u32[]{:S(2)}, u32[]{:S(2)}) collective-permute-start(bf16[2,192,1024]{2,1,0:T(8,128)(2,1)S(1)} %get-tuple-element.17), channel_id=1, source_target_pairs={{0,32},{32,64},{64,96},{96,0},{1,33},{33,65},{65,97},{97,1},{2,34}... | collective-permute-start | bytes 2359304 | tf_op jit(solution)/shard_map/ppermute | solution.py:236
  3.8 36.5 %collective-permute-start.4 = (bf16[2,192,1024]{2,1,0:T(8,128)(2,1)S(1)}, bf16[2,192,1024]{2,1,0:T(8,128)(2,1)S(1)}, u32[]{:S(2)}, u32[]{:S(2)}) collective-permute-start(bf16[2,192,1024]{2,1,0:T(8,128)(2,1)S(1)} %get-tuple-element.18), channel_id=1, source_target_pairs={{0,64},{32,96},{64,0},{96,32},{1,65},{33,97},{65,1},{97,33},{2,66}... | collective-permute-start | bytes 2359304 | tf_op jit(solution)/shard_map/ppermute | solution.py:236
  6.5 33.9 %copy-start = (s32[8]{0:T(128)S(1)}, s32[8]{0:T(128)}, u32[]{:S(2)}) copy-start(s32[8]{0:T(128)} %refs_0_.1) | copy-start | bytes 100
  6.5 33.9 %collective-permute-start.5 = (bf16[2,192,1024]{2,1,0:T(8,128)(2,1)S(1)}, bf16[2,192,1024]{2,1,0:T(8,128)(2,1)S(1)}, u32[]{:S(2)}, u32[]{:S(2)}) collective-permute-start(bf16[2,192,1024]{2,1,0:T(8,128)(2,1)S(1)} %get-tuple-element.19), channel_id=1, source_target_pairs={{0,96},{32,0},{64,32},{96,64},{1,97},{33,1},{65,33},{97,65},{2,98}... | collective-permute-start | bytes 2359304 | tf_op jit(solution)/shard_map/ppermute | solution.py:236
  8.7 36.2 %collective-permute-start = (bf16[2,64,1024]{2,1,0:T(8,128)(2,1)S(1)}, bf16[2,64,1024]{2,1,0:T(8,128)(2,1)S(1)}, u32[]{:S(2)}, u32[]{:S(2)}) collective-permute-start(bf16[2,64,1024]{2,1,0:T(8,128)(2,1)S(1)} %get-tuple-element.14), channel_id=1, source_target_pairs={{0,32},{32,64},{64,96},{96,0},{1,33},{33,65},{65,97},{97,1},{2,34}... | collective-permute-start | bytes 786440 | tf_op jit(solution)/shard_map/ppermute | solution.py:236
  9.2 42.4 %collective-permute-start.1 = (bf16[2,64,1024]{2,1,0:T(8,128)(2,1)S(1)}, bf16[2,64,1024]{2,1,0:T(8,128)(2,1)S(1)}, u32[]{:S(2)}, u32[]{:S(2)}) collective-permute-start(bf16[2,64,1024]{2,1,0:T(8,128)(2,1)S(1)} %get-tuple-element.15), channel_id=1, source_target_pairs={{0,64},{32,96},{64,0},{96,32},{1,65},{33,97},{65,1},{97,33},{2,66}... | collective-permute-start | bytes 786440 | tf_op jit(solution)/shard_map/ppermute | solution.py:236
  22.4 29.1 %collective-permute-start.2 = (bf16[2,64,1024]{2,1,0:T(8,128)(2,1)S(1)}, bf16[2,64,1024]{2,1,0:T(8,128)(2,1)S(1)}, u32[]{:S(2)}, u32[]{:S(2)}) collective-permute-start(bf16[2,64,1024]{2,1,0:T(8,128)(2,1)S(1)} %get-tuple-element.16), channel_id=1, source_target_pairs={{0,96},{32,0},{64,32},{96,64},{1,97},{33,1},{65,33},{97,65},{2,98}... | collective-permute-start | bytes 786440 | tf_op jit(solution)/shard_map/ppermute | solution.py:236

commit v3 on v2

v3 whole, which is shorter than its diff:
```python
import functools

import jax
import jax.numpy as jnp
from jax import lax
from jax.experimental import pallas as pl
from jax.experimental.pallas import tpu as pltpu
from jax.sharding import Mesh
from jax.sharding import PartitionSpec as P

PARAM = ("param_0", "param_1", "param_2")
TASK_PARAM = ("task", *PARAM)
CHUNKS = (192, 64)
SHIFTS = (2, 1, 3)
GROUPS = (((2, 0, 256), (1, 0, 192), (3, 0, 192)), ((1, 192, 64), (3, 192, 64)))
GRAIN = 16
OUT_ROWS = 64
LANES = 128
SUBLANES = 8
EPS = 1e-06
VMEM = pl.BlockSpec(memory_space=pltpu.VMEM)
SMEM = pl.BlockSpec(memory_space=pltpu.SMEM)


def slot_tasks(parts, per):
    me = lax.axis_index("task")
    return [lax.rem(me + (parts - s), parts) * per + u for s in (0, *SHIFTS) for u in range(per)]


def tables(order_ref, slots, rows_ref, columns_ref, pick_ref):
    tasks = len(slots)

    def ordered(shape, dim):
        place, task = lax.broadcasted_iota(jnp.int32, shape, dim), jnp.full(shape, -1, jnp.int32)
        for k in range(tasks):
            task = jnp.where(place == k, order_ref[k], task)
        return task

    lane = lax.broadcasted_iota(jnp.int32, rows_ref.shape, 1)
    rows_ref[...] = jnp.where(lane // tasks == ordered(rows_ref.shape, 0), 1.0, 0.0)
    sub = lax.broadcasted_iota(jnp.int32, columns_ref.shape, 0)
    columns_ref[...] = jnp.where(sub % tasks == ordered(columns_ref.shape, 1), 1.0, 0.0)
    for i, task in enumerate(slots):
        pick_ref[i] = jnp.where(ordered(pick_ref.shape[1:], 0) == task, 1.0, 0.0)


def pieces_of(value):
    high = value.astype(jnp.bfloat16)
    rest = value - high.astype(jnp.float32)
    middle = rest.astype(jnp.bfloat16)
    return high, middle, (rest - middle.astype(jnp.float32)).astype(jnp.bfloat16)


def exact_dot(x, y, contract):
    return lax.dot_general(x, y, (contract, ((), ())), preferred_element_type=jnp.float32)


def gram_kernel(parts, per, rows, bases, first, last, *refs):
    if first:
        order_ref, refs = refs[0], refs[1:]
    blocks, refs = refs[:parts], refs[parts:]
    if not first:
        before_ref, refs = refs[0], refs[1:]
    out_ref, *refs = refs
    acc_ref = refs[-1] if last else out_ref
    tasks = parts * per
    width = blocks[0].shape[2]
    slots = slot_tasks(parts, per)
    pairs = [(i, j) for i in range(tasks) for j in range(i, tasks)]

    def body(r, sums):
        sums = list(sums)
        for c in range(width // LANES):
            cols = pl.ds(c * LANES, LANES)
            x = [
                b[u, pl.ds(base + r * GRAIN, GRAIN), cols].astype(jnp.float32)
                for b, base in zip(blocks, bases)
                for u in range(per)
            ]
            for h in range(GRAIN // SUBLANES):
                part = [v[h * SUBLANES : (h + 1) * SUBLANES] for v in x]
                for p, (i, j) in enumerate(pairs):
                    sums[p] = sums[p] + part[i] * part[j]
        return tuple(sums)

    zero = jnp.zeros((SUBLANES, LANES), jnp.float32)
    sums = lax.fori_loop(0, rows // GRAIN, body, (zero,) * len(pairs))
    square = tasks * tasks
    for p, (i, j) in enumerate(pairs):
        for a, b in ((i, j), (j, i))[: 1 if i == j else 2]:
            acc_ref[pl.ds(slots[a] * tasks + slots[b], SUBLANES, stride=square), :] = sums[p]
    if not first:
        acc_ref[...] += before_ref[...]
    if first:
        tables(order_ref, slots, *refs[:3])
    if last:
        folded = acc_ref[:square, :]
        for k in range(1, SUBLANES):
            folded = folded + acc_ref[k * square : (k + 1) * square, :]
        high, middle, low = pieces_of(folded)
        ones = jnp.ones((GRAIN, LANES), jnp.bfloat16)
        row = exact_dot(ones, jnp.concatenate([high, middle], axis=0), ((1,), (1,)))
        row += exact_dot(ones, jnp.concatenate([jnp.zeros_like(low), low], axis=0), ((1,), (1,)))
        out_ref[...] = jnp.broadcast_to(row[:1], out_ref.shape)


def gram_of(order, chunk, rows, before, devices, last):
    blocks, bases = zip(*chunk)
    parts, per = len(blocks), blocks[0].shape[0]
    tasks = parts * per
    table = (SUBLANES * tasks**2, LANES)
    first = before is None
    shapes = [(devices, LANES) if last else table]
    if first:
        shapes += [(tasks, LANES), (LANES, LANES), (tasks, tasks, LANES)]
    return pl.pallas_call(
        functools.partial(gram_kernel, parts, per, rows, bases, first, last),
        in_specs=[SMEM] * first + [VMEM] * (parts + (not first)),
        out_specs=[VMEM] * len(shapes),
        out_shape=[jax.ShapeDtypeStruct(shape, jnp.float32) for shape in shapes],
        scratch_shapes=[pltpu.VMEM(table, jnp.float32)] if last else [],
        compiler_params=pltpu.CompilerParams(vmem_limit_bytes=4 << 20),
        name="gram",
    )(*([order] if first else []), *blocks, *([] if first else [before]))


def combine_kernel(per, entries, chunks, gram_ref, rows_ref, columns_ref, pick_ref, *refs):
    refs, (out_ref, total_ref, sems) = refs[:-3], refs[-3:]
    tasks = rows_ref.shape[0]
    flat = jnp.sum(gram_ref[...], axis=0, keepdims=True)
    flat = flat + pltpu.roll(flat, tasks * tasks, 1)
    pieces = [p.astype(jnp.float32) for p in pieces_of(flat)]
    spread = jnp.concatenate([rows_ref[...] * p for p in pieces], axis=0).astype(jnp.bfloat16)
    found = exact_dot(spread, columns_ref[...].astype(jnp.bfloat16), ((1,), (0,)))
    gram = found[2 * tasks :] + found[tasks : 2 * tasks] + found[:tasks]
    lane = lax.broadcasted_iota(jnp.int32, (tasks, LANES), 1)
    sub = lax.broadcasted_iota(jnp.int32, (tasks, LANES), 0)
    eye = lane == sub
    norm = jnp.sum(jnp.where(eye, gram, 0.0), axis=1, keepdims=True)
    inverse = jnp.broadcast_to(1.0 / (norm + EPS), (tasks, LANES))
    columns = [jnp.broadcast_to(gram[:, k : k + 1], (tasks, LANES)) for k in range(tasks)]
    coefs, dots = eye.astype(jnp.float32), gram
    for k in range(tasks):
        w = jnp.minimum(dots[k : k + 1, :], 0.0) * inverse[k : k + 1, :]
        w = jnp.broadcast_to(jnp.where(lane[:1] == k, 0.0, w), (tasks, LANES))
        coefs = coefs - jnp.where(sub == k, w, 0.0)
        dots = dots - columns[k] * w
    weight = jnp.sum(coefs, axis=1, keepdims=True)
    energy = jnp.sum(weight * jnp.sum(dots, axis=1, keepdims=True), axis=0, keepdims=True)
    rms = jnp.sqrt(jnp.maximum(energy, 0.0) / entries + EPS)
    weight = jnp.broadcast_to(weight * (0.5 / rms), (tasks, LANES))
    weights = [
        jnp.broadcast_to(jnp.sum(pick_ref[i] * weight, axis=0, keepdims=True), (GRAIN, LANES))
        for i in range(tasks)
    ]
    width = total_ref.shape[1]
    copies = []
    for row0, size, places_of in chunks:
        blocks = [(refs[k], base) for k, base in places_of]
        for top in range(0, size, OUT_ROWS):

            def body(r, _):
                at = pl.multiple_of(top + r * GRAIN, GRAIN)
                for c in range(0, width, LANES):
                    cols = pl.ds(c, LANES)
                    total = None
                    for i, weight in enumerate(weights):
                        block, base = blocks[i // per]
                        x = block[i % per, pl.ds(base + at, GRAIN), cols]
                        term = weight * x.astype(jnp.float32)
                        total = term if total is None else total + term
                    total_ref[pl.ds(row0 + at, GRAIN), cols] = total
                return 0

            lax.fori_loop(0, OUT_ROWS // GRAIN, body, 0)
            span = pl.ds(row0 + top, OUT_ROWS)
            copy = pltpu.make_async_copy(total_ref.at[span], out_ref.at[span], sems.at[len(copies)])
            copy.start()
            copies.append(copy)
    for copy in copies:
        copy.wait()


def combine(gram, tables_of, chunks, sizes, entries):
    blocks, layout, row0 = [], [], 0
    for chunk, size in zip(chunks, sizes):
        found = []
        for block, base in chunk:
            known = [k for k, b in enumerate(blocks) if b is block]
            if not known:
                blocks.append(block)
            found.append((known[0] if known else len(blocks) - 1, base))
        layout.append((row0, size, tuple(found)))
        row0 += size
    per, _, width = blocks[0].shape
    return pl.pallas_call(
        functools.partial(combine_kernel, per, entries, tuple(layout)),
        in_specs=[VMEM] * (1 + len(tables_of) + len(blocks)),
        out_specs=pl.BlockSpec(memory_space=pltpu.HBM),
        out_shape=jax.ShapeDtypeStruct((row0, width), jnp.float32),
        scratch_shapes=[
            pltpu.VMEM((row0, width), jnp.float32),
            pltpu.SemaphoreType.DMA((row0 // OUT_ROWS,)),
        ],
        compiler_params=pltpu.CompilerParams(vmem_limit_bytes=4 << 20),
        name="combine",
    )(gram, *tables_of, *blocks)


def cut_kernel(parts, pieces, grads_ref, *refs):
    outs, sems = refs[:-1], refs[-1]
    me = lax.axis_index("task")
    copies = []
    for k, (s, row0, size) in enumerate(pieces):
        block = outs[k].shape[-1]
        column = pl.multiple_of(lax.rem(me + s, parts) * block, block)
        source = grads_ref.at[:, pl.ds(row0, size), pl.ds(column, block)]
        copies.append(pltpu.make_async_copy(source, outs[k], sems.at[k]))
    for copy in copies:
        copy.start()
    for copy in copies:
        copy.wait()


def cut(grads, parts, pieces):
    per, _, width = grads.shape
    cuts = pl.pallas_call(
        functools.partial(cut_kernel, parts, pieces),
        in_specs=[pl.BlockSpec(memory_space=pltpu.HBM)],
        out_specs=[VMEM] * len(pieces),
        out_shape=[pltpu.VMEM((per, size, width // parts), grads.dtype) for _, _, size in pieces],
        scratch_shapes=[pltpu.SemaphoreType.DMA((len(pieces),))],
        compiler_params=pltpu.CompilerParams(vmem_limit_bytes=4 << 20),
        name="cut",
    )(pltpu.with_memory_space_constraint(grads, pltpu.HBM))
    return [near(c) for c in cuts]


def near(value):
    return pltpu.with_memory_space_constraint(value, pltpu.VMEM)


def shift(value, axis, by):
    n = lax.axis_size(axis)
    return near(lax.ppermute(value, axis, [(i, (i + by) % n) for i in range(n)]))


def shards(grads, order):
    per, rows, width = grads.shape
    parts, devices = lax.axis_size("task"), lax.axis_size(TASK_PARAM)
    entries = rows * lax.axis_size(PARAM) * width
    sent = {}
    for pieces in GROUPS:
        for piece, c in zip(pieces, cut(grads, parts, pieces)):
            sent[piece] = shift(c, "task", piece[0])
    own = cut(grads, parts, ((0, 0, rows),))[0]
    chunks, row0 = [], 0
    for size in CHUNKS:
        chunk = [(own, row0)]
        for s in SHIFTS:
            for (by, top, height), block in sent.items():
                if by == s and top <= row0 < top + height:
                    chunk.append((block, row0 - top))
        chunks.append(chunk)
        row0 += size
    gram, tables_of = None, None
    for k, (chunk, size) in enumerate(zip(chunks, CHUNKS)):
        gram, *more = gram_of(order, chunk, size, gram, devices, k == len(CHUNKS) - 1)
        tables_of = more or tables_of
    gram = lax.all_to_all(gram, TASK_PARAM, 0, 0, tiled=True)
    return combine(gram, tables_of, chunks, CHUNKS, entries)


def solution(mesh):
    torus = Mesh(
        mesh.devices.reshape(mesh.shape["task"], 4, 4, 2), ("task", "param_0", "param_1", "param_2")
    )
    in_specs = (P("task", PARAM, None), P())
    out_specs = P(PARAM, "task")
    return jax.shard_map(
        shards, mesh=torus, in_specs=in_specs, out_specs=out_specs, check_vma=False
    )
```

time: 75.2 us -> 74.7 us (level)
  starting transfers between devices: 8.44 us -> 9.24 us
    ppermute x6 -> x5, starting transfers between devices: 8.44 us -> 9.24 us  [shift(): lax.ppermute(value, axis, [(i, (i + by) % n) for i in range(n)])]
    ppermute x6 -> x5, waiting for transfers between devices: 36.2 us -> 35.5 us  [shift(): lax.ppermute(value, axis, [(i, (i + by) % n) for i in range(n)])]
  transfers between devices with their start and end apart: 6 -> 5, of which waited for: 4 -> 2; matrix products, arithmetic and copies ran while one was open for 0% -> 0% of each run, Pallas kernels for 7% -> 7%
where the time goes in v3:
time: 74.7 us; the launch traced here: 74.5 us
  waiting for transfers between devices  35.5 us (48%)
  blocking collectives  19.7 us (26%)
  Pallas kernels  10 us (13%)
  starting transfers between devices  9.24 us (12%)
    ppermute x5, waiting for transfers between devices, shift(): lax.ppermute(value, axis, [(i, (i + by) % n) for i in range(n)])  35.5 us
    all_to_all x1, blocking collectives, shards(): gram = lax.all_to_all(gram, TASK_PARAM, 0, 0, tiled=True)  19.7 us
    ppermute x5, starting transfers between devices, shift(): lax.ppermute(value, axis, [(i, (i + by) % n) for i in range(n)])  9.24 us
    pallas_call x3, Pallas kernels, cut(): pl.pallas_call(functools.partial(cut_kernel, parts, pieces), in_specs=[pl...  4 us
    pallas_call x2, Pallas kernels, gram_of(): pl.pallas_call(functools.partial(gram_kernel, parts, per, rows, bases, fi...  3.93 us
    pallas_call x1, Pallas kernels, combine(): pl.pallas_call(functools.partial(combine_kernel, per, entries, tuple(layo...  2.11 us
  transfers between devices with their start and end apart: 5, of which 2 were waited for; matrix products, arithmetic and copies ran while one was open for 0% of the time, Pallas kernels for 7%

profile of v3, /device:TPU:1, one launch (start us, length us, event | category | flops | bytes accessed | tf_op | source)
XLA Modules:
  0.0 74.5 jit_solution(9765501734908446878)
XLA Ops:
  0.0 1.7 %cut.4 = (bf16[2,256,1024]{2,1,0:T(8,128)(2,1)S(1)}, bf16[2,192,1024]{2,1,0:T(8,128)(2,1)S(1)}, bf16[2,192,1024]{2,1,0:T(8,128)(2,1)S(1)}) custom-call(bf16[2,256,4096]{2,1,0:T(8,128)(2,1)} %grads_ref.5), custom_call_target="tpu_custom_call" | custom-call | tf_op jit(solution)/shard_map/cut/pallas_call | solution.py:227
  1.7 3.8 %collective-permute-start = (bf16[2,256,1024]{2,1,0:T(8,128)(2,1)S(1)}, bf16[2,256,1024]{2,1,0:T(8,128)(2,1)S(1)}, u32[]{:S(2)}, u32[]{:S(2)}) collective-permute-start(bf16[2,256,1024]{2,1,0:T(8,128)(2,1)S(1)} %get-tuple-element.14), channel_id=1, source_target_pairs={{0,64},{32,96},{64,0},{96,32},{1,65},{33,97},{65,1},{97,33},{2,66}... | collective-permute-start | bytes 3145736 | tf_op jit(solution)/shard_map/ppermute | solution.py:245
  5.6 0.4 collective-permute-start.3
  6.0 0.0 copy-start
  6.0 2.3 %collective-permute-start.4 = (bf16[2,192,1024]{2,1,0:T(8,128)(2,1)S(1)}, bf16[2,192,1024]{2,1,0:T(8,128)(2,1)S(1)}, u32[]{:S(2)}, u32[]{:S(2)}) collective-permute-start(bf16[2,192,1024]{2,1,0:T(8,128)(2,1)S(1)} %get-tuple-element.18), channel_id=1, source_target_pairs={{0,96},{32,0},{64,32},{96,64},{1,97},{33,1},{65,33},{97,65},{2,98}... | collective-permute-start | bytes 2359304 | tf_op jit(solution)/shard_map/ppermute | solution.py:245
  8.2 1.0 %cut.5 = (bf16[2,64,1024]{2,1,0:T(8,128)(2,1)S(1)}, bf16[2,64,1024]{2,1,0:T(8,128)(2,1)S(1)}) custom-call(bf16[2,256,4096]{2,1,0:T(8,128)(2,1)} %grads_ref.5), custom_call_target="tpu_custom_call" | custom-call | tf_op jit(solution)/shard_map/cut/pallas_call | solution.py:227
  9.3 0.1 collective-permute-start.1
  9.4 2.7 %collective-permute-start.2 = (bf16[2,64,1024]{2,1,0:T(8,128)(2,1)S(1)}, bf16[2,64,1024]{2,1,0:T(8,128)(2,1)S(1)}, u32[]{:S(2)}, u32[]{:S(2)}) collective-permute-start(bf16[2,64,1024]{2,1,0:T(8,128)(2,1)S(1)} %get-tuple-element.16), channel_id=1, source_target_pairs={{0,96},{32,0},{64,32},{96,64},{1,97},{33,1},{65,33},{97,65},{2,98}... | collective-permute-start | bytes 786440 | tf_op jit(solution)/shard_map/ppermute | solution.py:245
  12.0 1.2 %cut.3.refs_1_.refs_0_ = bf16[2,256,1024]{2,1,0:T(8,128)(2,1)S(1)} custom-call(bf16[2,256,4096]{2,1,0:T(8,128)(2,1)} %grads_ref.5), custom_call_target="tpu_custom_call" | custom-call | tf_op jit(solution)/shard_map/cut/pallas_call | solution.py:227
  13.3 32.8 %collective-permute-done.3.refs_3_.refs_2_ = bf16[2,192,1024]{2,1,0:T(8,128)(2,1)S(1)} collective-permute-done((bf16[2,192,1024]{2,1,0:T(8,128)(2,1)S(1)}, bf16[2,192,1024]{2,1,0:T(8,128)(2,1)S(1)}, u32[]{:S(2)}, u32[]{:S(2)}) %collective-permute-start.3) | collective-permute-done | bytes 786464 | tf_op jit(solution)/shard_map/ppermute | solution.py:245
  46.0 0.0 collective-permute-done.4.refs_4_.refs_3_
  46.0 0.0 collective-permute-done.refs_2_.refs_1_
  46.0 0.0 copy-done
  46.0 2.9 %gram.2 = (f32[512,128]{1,0:T(8,128)S(1)}, f32[8,128]{1,0:T(8,128)S(1)}, f32[128,128]{1,0:T(8,128)S(1)}, f32[8,8,128]{2,1,0:T(8,128)S(1)}) custom-call(s32[8]{0:T(128)S(1)} %copy-done, bf16[2,256,1024]{2,1,0:T(8,128)(2,1)S(1)} %cut.3.refs_1_.refs_0_, bf16[2,256,1024]{2,1,0:T(8,128)(2,1)S(1)} %collective-permute-done.refs_2_.refs_1_, ...), custom_call_target="tpu_custom_call" | custom-call | tf_op jit(solution)/shard_map/gram/pallas_call | solution.py:116
  48.9 2.7 %collective-permute-done.1.refs_2_.refs_4_ = bf16[2,64,1024]{2,1,0:T(8,128)(2,1)S(1)} collective-permute-done((bf16[2,64,1024]{2,1,0:T(8,128)(2,1)S(1)}, bf16[2,64,1024]{2,1,0:T(8,128)(2,1)S(1)}, u32[]{:S(2)}, u32[]{:S(2)}) %collective-permute-start.1) | collective-permute-done | bytes 262176 | tf_op jit(solution)/shard_map/ppermute | solution.py:245
  51.6 0.0 collective-permute-done.2.refs_3_.refs_5_
  51.7 1.0 %gram.3 = f32[128,128]{1,0:T(8,128)S(1)} custom-call(bf16[2,256,1024]{2,1,0:T(8,128)(2,1)S(1)} %cut.3.refs_1_.refs_0_, bf16[2,256,1024]{2,1,0:T(8,128)(2,1)S(1)} %collective-permute-done.refs_2_.refs_1_, bf16[2,64,1024]{2,1,0:T(8,128)(2,1)S(1)} %collective-permute-done.1.refs_2_.refs_4_, bf16[2,64,1024]{2,1,0:T(8,128)(2,1)S(1)} %collective-permute-done.2.refs_3_.refs_5_, ...), custom_call_target="tpu_custom_call" | custom-call | tf_op jit(solution)/shard_map/gram/pallas_call | solution.py:116
  52.7 19.7 %all_to_all.11 = f32[128,1,128]{2,1,0:T(1,128)S(1)} all-to-all(f32[128,1,128]{2,1,0:T(1,128)S(1)} %bitcast.5), channel_id=1, replica_groups=mesh['task'=4,'param_0'=4,'param_1'=4,'param_2'=2] {'task','param_0','pa..., dimensions={0} | all-to-all | bytes 131072 | tf_op jit(solution)/shard_map/all_to_all | solution.py:270
  72.3 2.1 %combine.1 = f32[256,1024]{1,0:T(8,128)} custom-call(f32[128,128]{1,0:T(8,128)S(1)} %bitcast.4, f32[8,128]{1,0:T(8,128)S(1)} %get-tuple-element.20.rows_ref, f32[128,128]{1,0:T(8,128)S(1)} %get-tuple-element.21.columns_ref, f32[8,8,128]{2,1,0:T(8,128)S(1)} %get-tuple-element.22.pick_ref, bf16[2,256,1024]{2,1,0:T(8,128)(2,1)S(1)} %cut.3.refs_1_.refs_0_, ...), custom_call_target="tpu_custom_call" | custom-call | tf_op jit(solution)/shard_map/combine/pallas_call | solution.py:196
Async XLA Ops:
  1.7 44.3 %collective-permute-start = (bf16[2,256,1024]{2,1,0:T(8,128)(2,1)S(1)}, bf16[2,256,1024]{2,1,0:T(8,128)(2,1)S(1)}, u32[]{:S(2)}, u32[]{:S(2)}) collective-permute-start(bf16[2,256,1024]{2,1,0:T(8,128)(2,1)S(1)} %get-tuple-element.14), channel_id=1, source_target_pairs={{0,64},{32,96},{64,0},{96,32},{1,65},{33,97},{65,1},{97,33},{2,66}... | collective-permute-start | bytes 3145736 | tf_op jit(solution)/shard_map/ppermute | solution.py:245
  5.6 40.5 %collective-permute-start.3 = (bf16[2,192,1024]{2,1,0:T(8,128)(2,1)S(1)}, bf16[2,192,1024]{2,1,0:T(8,128)(2,1)S(1)}, u32[]{:S(2)}, u32[]{:S(2)}) collective-permute-start(bf16[2,192,1024]{2,1,0:T(8,128)(2,1)S(1)} %get-tuple-element.17), channel_id=1, source_target_pairs={{0,32},{32,64},{64,96},{96,0},{1,33},{33,65},{65,97},{97,1},{2,34}... | collective-permute-start | bytes 2359304 | tf_op jit(solution)/shard_map/ppermute | solution.py:245
  6.0 40.1 %copy-start = (s32[8]{0:T(128)S(1)}, s32[8]{0:T(128)}, u32[]{:S(2)}) copy-start(s32[8]{0:T(128)} %refs_0_.1) | copy-start | bytes 100
  6.0 40.1 %collective-permute-start.4 = (bf16[2,192,1024]{2,1,0:T(8,128)(2,1)S(1)}, bf16[2,192,1024]{2,1,0:T(8,128)(2,1)S(1)}, u32[]{:S(2)}, u32[]{:S(2)}) collective-permute-start(bf16[2,192,1024]{2,1,0:T(8,128)(2,1)S(1)} %get-tuple-element.18), channel_id=1, source_target_pairs={{0,96},{32,0},{64,32},{96,64},{1,97},{33,1},{65,33},{97,65},{2,98}... | collective-permute-start | bytes 2359304 | tf_op jit(solution)/shard_map/ppermute | solution.py:245
  9.3 42.4 %collective-permute-start.1 = (bf16[2,64,1024]{2,1,0:T(8,128)(2,1)S(1)}, bf16[2,64,1024]{2,1,0:T(8,128)(2,1)S(1)}, u32[]{:S(2)}, u32[]{:S(2)}) collective-permute-start(bf16[2,64,1024]{2,1,0:T(8,128)(2,1)S(1)} %get-tuple-element.15), channel_id=1, source_target_pairs={{0,32},{32,64},{64,96},{96,0},{1,33},{33,65},{65,97},{97,1},{2,34}... | collective-permute-start | bytes 786440 | tf_op jit(solution)/shard_map/ppermute | solution.py:245
  9.4 42.3 %collective-permute-start.2 = (bf16[2,64,1024]{2,1,0:T(8,128)(2,1)S(1)}, bf16[2,64,1024]{2,1,0:T(8,128)(2,1)S(1)}, u32[]{:S(2)}, u32[]{:S(2)}) collective-permute-start(bf16[2,64,1024]{2,1,0:T(8,128)(2,1)S(1)} %get-tuple-element.16), channel_id=1, source_target_pairs={{0,96},{32,0},{64,32},{96,64},{1,97},{33,1},{65,33},{97,65},{2,98}... | collective-permute-start | bytes 786440 | tf_op jit(solution)/shard_map/ppermute | solution.py:245

commit v4 on v3

--- a/solution.py
+++ b/solution.py
@@ -18,6 +18,7 @@
 LANES = 128
 SUBLANES = 8
 EPS = 1e-06
+CANCEL = 0.001
 VMEM = pl.BlockSpec(memory_space=pltpu.VMEM)
 SMEM = pl.BlockSpec(memory_space=pltpu.SMEM)
 
@@ -125,7 +126,7 @@
 
 
 def combine_kernel(per, entries, chunks, gram_ref, rows_ref, columns_ref, pick_ref, *refs):
-    refs, (out_ref, total_ref, sems) = refs[:-3], refs[-3:]
+    refs, (out_ref, stats_ref, total_ref, sems) = refs[:-4], refs[-4:]
     tasks = rows_ref.shape[0]
     flat = jnp.sum(gram_ref[...], axis=0, keepdims=True)
     flat = flat + pltpu.roll(flat, tasks * tasks, 1)
@@ -147,8 +148,12 @@
         dots = dots - columns[k] * w
     weight = jnp.sum(coefs, axis=1, keepdims=True)
     energy = jnp.sum(weight * jnp.sum(dots, axis=1, keepdims=True), axis=0, keepdims=True)
-    rms = jnp.sqrt(jnp.maximum(energy, 0.0) / entries + EPS)
-    weight = jnp.broadcast_to(weight * (0.5 / rms), (tasks, LANES))
+    least = jnp.sum(jnp.abs(weight) * jnp.sqrt(jnp.maximum(norm, 0.0)), axis=0, keepdims=True)
+    least = least * least * CANCEL
+    scale = 0.5 / jnp.sqrt(jnp.maximum(energy, least) / entries + EPS)
+    stats_ref[0] = jnp.max(least - energy)
+    stats_ref[1] = jnp.max(scale)
+    weight = jnp.broadcast_to(weight * scale, (tasks, LANES))
     weights = [
         jnp.broadcast_to(jnp.sum(pick_ref[i] * weight, axis=0, keepdims=True), (GRAIN, LANES))
         for i in range(tasks)
@@ -196,8 +201,11 @@
     return pl.pallas_call(
         functools.partial(combine_kernel, per, entries, tuple(layout)),
         in_specs=[VMEM] * (1 + len(tables_of) + len(blocks)),
-        out_specs=pl.BlockSpec(memory_space=pltpu.HBM),
-        out_shape=jax.ShapeDtypeStruct((row0, width), jnp.float32),
+        out_specs=[pl.BlockSpec(memory_space=pltpu.HBM), SMEM],
+        out_shape=[
+            pltpu.HBM((row0, width), jnp.float32),
+            jax.ShapeDtypeStruct((2,), jnp.float32),
+        ],
         scratch_shapes=[
             pltpu.VMEM((row0, width), jnp.float32),
             pltpu.SemaphoreType.DMA((row0 // OUT_ROWS,)),
@@ -268,7 +276,13 @@
         gram, *more = gram_of(order, chunk, size, gram, devices, k == len(CHUNKS) - 1)
         tables_of = more or tables_of
     gram = lax.all_to_all(gram, TASK_PARAM, 0, 0, tiled=True)
-    return combine(gram, tables_of, chunks, CHUNKS, entries)
+    update, stats = combine(gram, tables_of, chunks, CHUNKS, entries)
+
+    def normalize(update):
+        energy = functools.reduce(lax.psum, TASK_PARAM, jnp.sum(update * update))
+        return update * (0.5 / jnp.sqrt(energy / entries + EPS * stats[1] * stats[1]))
+
+    return lax.cond(stats[0] > 0.0, normalize, lambda update: update, update)
 
 
 def solution(mesh):

time: 74.7 us -> 75.3 us (level)
  no operation moved by 1% of the time
where the time goes in v4:
time: 75.3 us; the launch traced here: 75.1 us
  waiting for transfers between devices  35.5 us (47%)
  blocking collectives  19.7 us (26%)
  Pallas kernels  10.7 us (14%)
  starting transfers between devices  9.24 us (12%)
    ppermute x5, waiting for transfers between devices, shift(): lax.ppermute(value, axis, [(i, (i + by) % n) for i in range(n)])  35.5 us
    all_to_all x1, blocking collectives, shards(): gram = lax.all_to_all(gram, TASK_PARAM, 0, 0, tiled=True)  19.7 us
    ppermute x5, starting transfers between devices, shift(): lax.ppermute(value, axis, [(i, (i + by) % n) for i in range(n)])  9.24 us
    pallas_call x3, Pallas kernels, cut(): pl.pallas_call(functools.partial(cut_kernel, parts, pieces), in_specs=[pl...  4 us
    pallas_call x2, Pallas kernels, gram_of(): pl.pallas_call(functools.partial(gram_kernel, parts, per, rows, bases, fi...  3.93 us
    pallas_call x1, Pallas kernels, combine(): pl.pallas_call(functools.partial(combine_kernel, per, entries, tuple(layo...  2.73 us
  transfers between devices with their start and end apart: 5, of which 2 were waited for; matrix products, arithmetic and copies ran while one was open for 0% of the time, Pallas kernels for 7%

profile of v4, /device:TPU:1, one launch (start us, length us, event | category | flops | bytes accessed | tf_op | source)
XLA Modules:
  0.0 75.1 jit_solution(10892751868672899439)
XLA Ops:
  0.0 1.7 %cut.4 = (bf16[2,256,1024]{2,1,0:T(8,128)(2,1)S(1)}, bf16[2,192,1024]{2,1,0:T(8,128)(2,1)S(1)}, bf16[2,192,1024]{2,1,0:T(8,128)(2,1)S(1)}) custom-call(bf16[2,256,4096]{2,1,0:T(8,128)(2,1)} %grads_ref.5), custom_call_target="tpu_custom_call" | custom-call | tf_op jit(solution)/shard_map/cut/pallas_call | solution.py:235
  1.7 3.8 %collective-permute-start = (bf16[2,256,1024]{2,1,0:T(8,128)(2,1)S(1)}, bf16[2,256,1024]{2,1,0:T(8,128)(2,1)S(1)}, u32[]{:S(2)}, u32[]{:S(2)}) collective-permute-start(bf16[2,256,1024]{2,1,0:T(8,128)(2,1)S(1)} %get-tuple-element.26), channel_id=1, source_target_pairs={{0,64},{32,96},{64,0},{96,32},{1,65},{33,97},{65,1},{97,33},{2,66}... | collective-permute-start | bytes 3145736 | tf_op jit(solution)/shard_map/ppermute | solution.py:253
  5.6 0.4 collective-permute-start.3
  6.0 0.0 copy-start
  6.0 2.3 %collective-permute-start.4 = (bf16[2,192,1024]{2,1,0:T(8,128)(2,1)S(1)}, bf16[2,192,1024]{2,1,0:T(8,128)(2,1)S(1)}, u32[]{:S(2)}, u32[]{:S(2)}) collective-permute-start(bf16[2,192,1024]{2,1,0:T(8,128)(2,1)S(1)} %get-tuple-element.30), channel_id=1, source_target_pairs={{0,96},{32,0},{64,32},{96,64},{1,97},{33,1},{65,33},{97,65},{2,98}... | collective-permute-start | bytes 2359304 | tf_op jit(solution)/shard_map/ppermute | solution.py:253
  8.2 1.0 %cut.5 = (bf16[2,64,1024]{2,1,0:T(8,128)(2,1)S(1)}, bf16[2,64,1024]{2,1,0:T(8,128)(2,1)S(1)}) custom-call(bf16[2,256,4096]{2,1,0:T(8,128)(2,1)} %grads_ref.5), custom_call_target="tpu_custom_call" | custom-call | tf_op jit(solution)/shard_map/cut/pallas_call | solution.py:235
  9.3 0.1 collective-permute-start.1
  9.4 2.7 %collective-permute-start.2 = (bf16[2,64,1024]{2,1,0:T(8,128)(2,1)S(1)}, bf16[2,64,1024]{2,1,0:T(8,128)(2,1)S(1)}, u32[]{:S(2)}, u32[]{:S(2)}) collective-permute-start(bf16[2,64,1024]{2,1,0:T(8,128)(2,1)S(1)} %get-tuple-element.28), channel_id=1, source_target_pairs={{0,96},{32,0},{64,32},{96,64},{1,97},{33,1},{65,33},{97,65},{2,98}... | collective-permute-start | bytes 786440 | tf_op jit(solution)/shard_map/ppermute | solution.py:253
  12.0 1.2 %cut.3.refs_1_.refs_0_ = bf16[2,256,1024]{2,1,0:T(8,128)(2,1)S(1)} custom-call(bf16[2,256,4096]{2,1,0:T(8,128)(2,1)} %grads_ref.5), custom_call_target="tpu_custom_call" | custom-call | tf_op jit(solution)/shard_map/cut/pallas_call | solution.py:235
  13.3 32.8 %collective-permute-done.3.refs_3_.refs_2_ = bf16[2,192,1024]{2,1,0:T(8,128)(2,1)S(1)} collective-permute-done((bf16[2,192,1024]{2,1,0:T(8,128)(2,1)S(1)}, bf16[2,192,1024]{2,1,0:T(8,128)(2,1)S(1)}, u32[]{:S(2)}, u32[]{:S(2)}) %collective-permute-start.3) | collective-permute-done | bytes 786464 | tf_op jit(solution)/shard_map/ppermute | solution.py:253
  46.0 0.0 collective-permute-done.4.refs_4_.refs_3_
  46.0 0.0 collective-permute-done.refs_2_.refs_1_
  46.0 0.0 copy-done
  46.0 2.9 %gram.2 = (f32[512,128]{1,0:T(8,128)S(1)}, f32[8,128]{1,0:T(8,128)S(1)}, f32[128,128]{1,0:T(8,128)S(1)}, f32[8,8,128]{2,1,0:T(8,128)S(1)}) custom-call(s32[8]{0:T(128)S(1)} %copy-done, bf16[2,256,1024]{2,1,0:T(8,128)(2,1)S(1)} %cut.3.refs_1_.refs_0_, bf16[2,256,1024]{2,1,0:T(8,128)(2,1)S(1)} %collective-permute-done.refs_2_.refs_1_, ...), custom_call_target="tpu_custom_call" | custom-call | tf_op jit(solution)/shard_map/gram/pallas_call | solution.py:117
  48.9 2.7 %collective-permute-done.1.refs_2_.refs_4_ = bf16[2,64,1024]{2,1,0:T(8,128)(2,1)S(1)} collective-permute-done((bf16[2,64,1024]{2,1,0:T(8,128)(2,1)S(1)}, bf16[2,64,1024]{2,1,0:T(8,128)(2,1)S(1)}, u32[]{:S(2)}, u32[]{:S(2)}) %collective-permute-start.1) | collective-permute-done | bytes 262176 | tf_op jit(solution)/shard_map/ppermute | solution.py:253
  51.6 0.0 collective-permute-done.2.refs_3_.refs_5_
  51.7 1.0 %gram.3 = f32[128,128]{1,0:T(8,128)S(1)} custom-call(bf16[2,256,1024]{2,1,0:T(8,128)(2,1)S(1)} %cut.3.refs_1_.refs_0_, bf16[2,256,1024]{2,1,0:T(8,128)(2,1)S(1)} %collective-permute-done.refs_2_.refs_1_, bf16[2,64,1024]{2,1,0:T(8,128)(2,1)S(1)} %collective-permute-done.1.refs_2_.refs_4_, bf16[2,64,1024]{2,1,0:T(8,128)(2,1)S(1)} %collective-permute-done.2.refs_3_.refs_5_, ...), custom_call_target="tpu_custom_call" | custom-call | tf_op jit(solution)/shard_map/gram/pallas_call | solution.py:117
  52.7 19.7 %all_to_all.11 = f32[128,1,128]{2,1,0:T(1,128)S(1)} all-to-all(f32[128,1,128]{2,1,0:T(1,128)S(1)} %bitcast.8), channel_id=1, replica_groups=mesh['task'=4,'param_0'=4,'param_1'=4,'param_2'=2] {'task','param_0','pa..., dimensions={0} | all-to-all | bytes 131072 | tf_op jit(solution)/shard_map/all_to_all | solution.py:278
  72.3 2.7 %combine.1 = (f32[256,1024]{1,0:T(8,128)}, f32[2]{0:T(128)S(1)}) custom-call(f32[128,128]{1,0:T(8,128)S(1)} %bitcast.7, f32[8,128]{1,0:T(8,128)S(1)} %get-tuple-element.32.rows_ref, f32[128,128]{1,0:T(8,128)S(1)} %get-tuple-element.33.columns_ref, f32[8,8,128]{2,1,0:T(8,128)S(1)} %get-tuple-element.34.pick_ref, ...), custom_call_target="tpu_custom_call" | custom-call | tf_op jit(solution)/shard_map/combine/pallas_call | solution.py:201
  (1 shorter events, 0.0 us)
Async XLA Ops:
  1.7 44.3 %collective-permute-start = (bf16[2,256,1024]{2,1,0:T(8,128)(2,1)S(1)}, bf16[2,256,1024]{2,1,0:T(8,128)(2,1)S(1)}, u32[]{:S(2)}, u32[]{:S(2)}) collective-permute-start(bf16[2,256,1024]{2,1,0:T(8,128)(2,1)S(1)} %get-tuple-element.26), channel_id=1, source_target_pairs={{0,64},{32,96},{64,0},{96,32},{1,65},{33,97},{65,1},{97,33},{2,66}... | collective-permute-start | bytes 3145736 | tf_op jit(solution)/shard_map/ppermute | solution.py:253
  5.6 40.5 %collective-permute-start.3 = (bf16[2,192,1024]{2,1,0:T(8,128)(2,1)S(1)}, bf16[2,192,1024]{2,1,0:T(8,128)(2,1)S(1)}, u32[]{:S(2)}, u32[]{:S(2)}) collective-permute-start(bf16[2,192,1024]{2,1,0:T(8,128)(2,1)S(1)} %get-tuple-element.29), channel_id=1, source_target_pairs={{0,32},{32,64},{64,96},{96,0},{1,33},{33,65},{65,97},{97,1},{2,34}... | collective-permute-start | bytes 2359304 | tf_op jit(solution)/shard_map/ppermute | solution.py:253
  6.0 40.1 %copy-start = (s32[8]{0:T(128)S(1)}, s32[8]{0:T(128)}, u32[]{:S(2)}) copy-start(s32[8]{0:T(128)} %refs_0_.1) | copy-start | bytes 100
  6.0 40.1 %collective-permute-start.4 = (bf16[2,192,1024]{2,1,0:T(8,128)(2,1)S(1)}, bf16[2,192,1024]{2,1,0:T(8,128)(2,1)S(1)}, u32[]{:S(2)}, u32[]{:S(2)}) collective-permute-start(bf16[2,192,1024]{2,1,0:T(8,128)(2,1)S(1)} %get-tuple-element.30), channel_id=1, source_target_pairs={{0,96},{32,0},{64,32},{96,64},{1,97},{33,1},{65,33},{97,65},{2,98}... | collective-permute-start | bytes 2359304 | tf_op jit(solution)/shard_map/ppermute | solution.py:253
  9.3 42.4 %collective-permute-start.1 = (bf16[2,64,1024]{2,1,0:T(8,128)(2,1)S(1)}, bf16[2,64,1024]{2,1,0:T(8,128)(2,1)S(1)}, u32[]{:S(2)}, u32[]{:S(2)}) collective-permute-start(bf16[2,64,1024]{2,1,0:T(8,128)(2,1)S(1)} %get-tuple-element.27), channel_id=1, source_target_pairs={{0,32},{32,64},{64,96},{96,0},{1,33},{33,65},{65,97},{97,1},{2,34}... | collective-permute-start | bytes 786440 | tf_op jit(solution)/shard_map/ppermute | solution.py:253
  9.4 42.3 %collective-permute-start.2 = (bf16[2,64,1024]{2,1,0:T(8,128)(2,1)S(1)}, bf16[2,64,1024]{2,1,0:T(8,128)(2,1)S(1)}, u32[]{:S(2)}, u32[]{:S(2)}) collective-permute-start(bf16[2,64,1024]{2,1,0:T(8,128)(2,1)S(1)} %get-tuple-element.28), channel_id=1, source_target_pairs={{0,96},{32,0},{64,32},{96,64},{1,97},{33,1},{65,33},{97,65},{2,98}... | collective-permute-start | bytes 786440 | tf_op jit(solution)/shard_map/ppermute | solution.py:253

commit v5 on v4

--- a/solution.py
+++ b/solution.py
@@ -126,7 +126,7 @@
 
 
 def combine_kernel(per, entries, chunks, gram_ref, rows_ref, columns_ref, pick_ref, *refs):
-    refs, (out_ref, stats_ref, total_ref, sems) = refs[:-4], refs[-4:]
+    refs, (out_ref, poor_ref, scale_ref, total_ref, sems) = refs[:-5], refs[-5:]
     tasks = rows_ref.shape[0]
     flat = jnp.sum(gram_ref[...], axis=0, keepdims=True)
     flat = flat + pltpu.roll(flat, tasks * tasks, 1)
@@ -151,8 +151,8 @@
     least = jnp.sum(jnp.abs(weight) * jnp.sqrt(jnp.maximum(norm, 0.0)), axis=0, keepdims=True)
     least = least * least * CANCEL
     scale = 0.5 / jnp.sqrt(jnp.maximum(energy, least) / entries + EPS)
-    stats_ref[0] = jnp.max(least - energy)
-    stats_ref[1] = jnp.max(scale)
+    poor_ref[...] = jnp.broadcast_to(least - energy, (1, LANES)).reshape(LANES)
+    scale_ref[...] = jnp.broadcast_to(scale, (1, LANES)).reshape(LANES)
     weight = jnp.broadcast_to(weight * scale, (tasks, LANES))
     weights = [
         jnp.broadcast_to(jnp.sum(pick_ref[i] * weight, axis=0, keepdims=True), (GRAIN, LANES))
@@ -201,10 +201,11 @@
     return pl.pallas_call(
         functools.partial(combine_kernel, per, entries, tuple(layout)),
         in_specs=[VMEM] * (1 + len(tables_of) + len(blocks)),
-        out_specs=[pl.BlockSpec(memory_space=pltpu.HBM), SMEM],
+        out_specs=[pl.BlockSpec(memory_space=pltpu.HBM), VMEM, VMEM],
         out_shape=[
             pltpu.HBM((row0, width), jnp.float32),
-            jax.ShapeDtypeStruct((2,), jnp.float32),
+            jax.ShapeDtypeStruct((LANES,), jnp.float32),
+            jax.ShapeDtypeStruct((LANES,), jnp.float32),
         ],
         scratch_shapes=[
             pltpu.VMEM((row0, width), jnp.float32),
@@ -276,13 +277,13 @@
         gram, *more = gram_of(order, chunk, size, gram, devices, k == len(CHUNKS) - 1)
         tables_of = more or tables_of
     gram = lax.all_to_all(gram, TASK_PARAM, 0, 0, tiled=True)
-    update, stats = combine(gram, tables_of, chunks, CHUNKS, entries)
+    update, poor, scale = combine(gram, tables_of, chunks, CHUNKS, entries)
 
     def normalize(update):
         energy = functools.reduce(lax.psum, TASK_PARAM, jnp.sum(update * update))
-        return update * (0.5 / jnp.sqrt(energy / entries + EPS * stats[1] * stats[1]))
-
-    return lax.cond(stats[0] > 0.0, normalize, lambda update: update, update)
+        return update * (0.5 / jnp.sqrt(energy / entries + EPS * scale[0] * scale[0]))
+
+    return lax.cond(poor[0] > 0.0, normalize, lambda update: update, update)
 
 
 def solution(mesh):

time: 75.3 us -> 74.7 us (level)
  no operation moved by 1% of the time
where the time goes in v5:
time: 74.7 us; the launch traced here: 74.5 us
  waiting for transfers between devices  35.5 us (48%)
  blocking collectives  19.7 us (26%)
  Pallas kernels  10 us (13%)
  starting transfers between devices  9.24 us (12%)
    ppermute x5, waiting for transfers between devices, shift(): lax.ppermute(value, axis, [(i, (i + by) % n) for i in range(n)])  35.5 us
    all_to_all x1, blocking collectives, shards(): gram = lax.all_to_all(gram, TASK_PARAM, 0, 0, tiled=True)  19.7 us
    ppermute x5, starting transfers between devices, shift(): lax.ppermute(value, axis, [(i, (i + by) % n) for i in range(n)])  9.24 us
    pallas_call x3, Pallas kernels, cut(): pl.pallas_call(functools.partial(cut_kernel, parts, pieces), in_specs=[pl...  4 us
    pallas_call x2, Pallas kernels, gram_of(): pl.pallas_call(functools.partial(gram_kernel, parts, per, rows, bases, fi...  3.93 us
    pallas_call x1, Pallas kernels, combine(): pl.pallas_call(functools.partial(combine_kernel, per, entries, tuple(layo...  2.11 us
  transfers between devices with their start and end apart: 5, of which 2 were waited for; matrix products, arithmetic and copies ran while one was open for 0% of the time, Pallas kernels for 7%

profile of v5, /device:TPU:1, one launch (start us, length us, event | category | flops | bytes accessed | tf_op | source)
XLA Modules:
  0.0 74.5 jit_solution(16855370304936283071)
XLA Ops:
  0.0 1.7 %cut.4 = (bf16[2,256,1024]{2,1,0:T(8,128)(2,1)S(1)}, bf16[2,192,1024]{2,1,0:T(8,128)(2,1)S(1)}, bf16[2,192,1024]{2,1,0:T(8,128)(2,1)S(1)}) custom-call(bf16[2,256,4096]{2,1,0:T(8,128)(2,1)} %grads_ref.5), custom_call_target="tpu_custom_call" | custom-call | tf_op jit(solution)/shard_map/cut/pallas_call | solution.py:236
  1.7 3.8 %collective-permute-start = (bf16[2,256,1024]{2,1,0:T(8,128)(2,1)S(1)}, bf16[2,256,1024]{2,1,0:T(8,128)(2,1)S(1)}, u32[]{:S(2)}, u32[]{:S(2)}) collective-permute-start(bf16[2,256,1024]{2,1,0:T(8,128)(2,1)S(1)} %get-tuple-element.27), channel_id=1, source_target_pairs={{0,64},{32,96},{64,0},{96,32},{1,65},{33,97},{65,1},{97,33},{2,66}... | collective-permute-start | bytes 3145736 | tf_op jit(solution)/shard_map/ppermute | solution.py:254
  5.6 0.4 collective-permute-start.3
  6.0 0.0 copy-start
  6.0 2.3 %collective-permute-start.4 = (bf16[2,192,1024]{2,1,0:T(8,128)(2,1)S(1)}, bf16[2,192,1024]{2,1,0:T(8,128)(2,1)S(1)}, u32[]{:S(2)}, u32[]{:S(2)}) collective-permute-start(bf16[2,192,1024]{2,1,0:T(8,128)(2,1)S(1)} %get-tuple-element.31), channel_id=1, source_target_pairs={{0,96},{32,0},{64,32},{96,64},{1,97},{33,1},{65,33},{97,65},{2,98}... | collective-permute-start | bytes 2359304 | tf_op jit(solution)/shard_map/ppermute | solution.py:254
  8.2 1.0 %cut.5 = (bf16[2,64,1024]{2,1,0:T(8,128)(2,1)S(1)}, bf16[2,64,1024]{2,1,0:T(8,128)(2,1)S(1)}) custom-call(bf16[2,256,4096]{2,1,0:T(8,128)(2,1)} %grads_ref.5), custom_call_target="tpu_custom_call" | custom-call | tf_op jit(solution)/shard_map/cut/pallas_call | solution.py:236
  9.3 0.1 collective-permute-start.1
  9.4 2.7 %collective-permute-start.2 = (bf16[2,64,1024]{2,1,0:T(8,128)(2,1)S(1)}, bf16[2,64,1024]{2,1,0:T(8,128)(2,1)S(1)}, u32[]{:S(2)}, u32[]{:S(2)}) collective-permute-start(bf16[2,64,1024]{2,1,0:T(8,128)(2,1)S(1)} %get-tuple-element.29), channel_id=1, source_target_pairs={{0,96},{32,0},{64,32},{96,64},{1,97},{33,1},{65,33},{97,65},{2,98}... | collective-permute-start | bytes 786440 | tf_op jit(solution)/shard_map/ppermute | solution.py:254
  12.0 1.2 %cut.3.refs_1_.refs_0_ = bf16[2,256,1024]{2,1,0:T(8,128)(2,1)S(1)} custom-call(bf16[2,256,4096]{2,1,0:T(8,128)(2,1)} %grads_ref.5), custom_call_target="tpu_custom_call" | custom-call | tf_op jit(solution)/shard_map/cut/pallas_call | solution.py:236
  13.3 32.8 %collective-permute-done.3.refs_3_.refs_2_ = bf16[2,192,1024]{2,1,0:T(8,128)(2,1)S(1)} collective-permute-done((bf16[2,192,1024]{2,1,0:T(8,128)(2,1)S(1)}, bf16[2,192,1024]{2,1,0:T(8,128)(2,1)S(1)}, u32[]{:S(2)}, u32[]{:S(2)}) %collective-permute-start.3) | collective-permute-done | bytes 786464 | tf_op jit(solution)/shard_map/ppermute | solution.py:254
  46.0 0.0 collective-permute-done.4.refs_4_.refs_3_
  46.0 0.0 collective-permute-done.refs_2_.refs_1_
  46.0 0.0 copy-done
  46.0 2.9 %gram.2 = (f32[512,128]{1,0:T(8,128)S(1)}, f32[8,128]{1,0:T(8,128)S(1)}, f32[128,128]{1,0:T(8,128)S(1)}, f32[8,8,128]{2,1,0:T(8,128)S(1)}) custom-call(s32[8]{0:T(128)S(1)} %copy-done, bf16[2,256,1024]{2,1,0:T(8,128)(2,1)S(1)} %cut.3.refs_1_.refs_0_, bf16[2,256,1024]{2,1,0:T(8,128)(2,1)S(1)} %collective-permute-done.refs_2_.refs_1_, ...), custom_call_target="tpu_custom_call" | custom-call | tf_op jit(solution)/shard_map/gram/pallas_call | solution.py:117
  48.9 2.7 %collective-permute-done.1.refs_2_.refs_4_ = bf16[2,64,1024]{2,1,0:T(8,128)(2,1)S(1)} collective-permute-done((bf16[2,64,1024]{2,1,0:T(8,128)(2,1)S(1)}, bf16[2,64,1024]{2,1,0:T(8,128)(2,1)S(1)}, u32[]{:S(2)}, u32[]{:S(2)}) %collective-permute-start.1) | collective-permute-done | bytes 262176 | tf_op jit(solution)/shard_map/ppermute | solution.py:254
  51.6 0.0 collective-permute-done.2.refs_3_.refs_5_
  51.7 1.0 %gram.3 = f32[128,128]{1,0:T(8,128)S(1)} custom-call(bf16[2,256,1024]{2,1,0:T(8,128)(2,1)S(1)} %cut.3.refs_1_.refs_0_, bf16[2,256,1024]{2,1,0:T(8,128)(2,1)S(1)} %collective-permute-done.refs_2_.refs_1_, bf16[2,64,1024]{2,1,0:T(8,128)(2,1)S(1)} %collective-permute-done.1.refs_2_.refs_4_, bf16[2,64,1024]{2,1,0:T(8,128)(2,1)S(1)} %collective-permute-done.2.refs_3_.refs_5_, ...), custom_call_target="tpu_custom_call" | custom-call | tf_op jit(solution)/shard_map/gram/pallas_call | solution.py:117
  52.7 19.7 %all_to_all.11 = f32[128,1,128]{2,1,0:T(1,128)S(1)} all-to-all(f32[128,1,128]{2,1,0:T(1,128)S(1)} %bitcast.9), channel_id=1, replica_groups=mesh['task'=4,'param_0'=4,'param_1'=4,'param_2'=2] {'task','param_0','pa..., dimensions={0} | all-to-all | bytes 131072 | tf_op jit(solution)/shard_map/all_to_all | solution.py:279
  72.3 2.1 %combine.1 = (f32[256,1024]{1,0:T(8,128)}, f32[128]{0:T(128)S(1)}, f32[128]{0:T(128)S(1)}) custom-call(f32[128,128]{1,0:T(8,128)S(1)} %bitcast.8, f32[8,128]{1,0:T(8,128)S(1)} %get-tuple-element.33.rows_ref, f32[128,128]{1,0:T(8,128)S(1)} %get-tuple-element.34.columns_ref, f32[8,8,128]{2,1,0:T(8,128)S(1)} %get-tuple-element.35.pick_ref, ...), custom_call_target="tpu_custom_call" | custom-call | tf_op jit(solution)/shard_map/combine/pallas_call | solution.py:201
  (1 shorter events, 0.0 us)
Async XLA Ops:
  1.7 44.3 %collective-permute-start = (bf16[2,256,1024]{2,1,0:T(8,128)(2,1)S(1)}, bf16[2,256,1024]{2,1,0:T(8,128)(2,1)S(1)}, u32[]{:S(2)}, u32[]{:S(2)}) collective-permute-start(bf16[2,256,1024]{2,1,0:T(8,128)(2,1)S(1)} %get-tuple-element.27), channel_id=1, source_target_pairs={{0,64},{32,96},{64,0},{96,32},{1,65},{33,97},{65,1},{97,33},{2,66}... | collective-permute-start | bytes 3145736 | tf_op jit(solution)/shard_map/ppermute | solution.py:254
  5.6 40.5 %collective-permute-start.3 = (bf16[2,192,1024]{2,1,0:T(8,128)(2,1)S(1)}, bf16[2,192,1024]{2,1,0:T(8,128)(2,1)S(1)}, u32[]{:S(2)}, u32[]{:S(2)}) collective-permute-start(bf16[2,192,1024]{2,1,0:T(8,128)(2,1)S(1)} %get-tuple-element.30), channel_id=1, source_target_pairs={{0,32},{32,64},{64,96},{96,0},{1,33},{33,65},{65,97},{97,1},{2,34}... | collective-permute-start | bytes 2359304 | tf_op jit(solution)/shard_map/ppermute | solution.py:254
  6.0 40.1 %copy-start = (s32[8]{0:T(128)S(1)}, s32[8]{0:T(128)}, u32[]{:S(2)}) copy-start(s32[8]{0:T(128)} %refs_0_.1) | copy-start | bytes 100
  6.0 40.1 %collective-permute-start.4 = (bf16[2,192,1024]{2,1,0:T(8,128)(2,1)S(1)}, bf16[2,192,1024]{2,1,0:T(8,128)(2,1)S(1)}, u32[]{:S(2)}, u32[]{:S(2)}) collective-permute-start(bf16[2,192,1024]{2,1,0:T(8,128)(2,1)S(1)} %get-tuple-element.31), channel_id=1, source_target_pairs={{0,96},{32,0},{64,32},{96,64},{1,97},{33,1},{65,33},{97,65},{2,98}... | collective-permute-start | bytes 2359304 | tf_op jit(solution)/shard_map/ppermute | solution.py:254
  9.3 42.4 %collective-permute-start.1 = (bf16[2,64,1024]{2,1,0:T(8,128)(2,1)S(1)}, bf16[2,64,1024]{2,1,0:T(8,128)(2,1)S(1)}, u32[]{:S(2)}, u32[]{:S(2)}) collective-permute-start(bf16[2,64,1024]{2,1,0:T(8,128)(2,1)S(1)} %get-tuple-element.28), channel_id=1, source_target_pairs={{0,32},{32,64},{64,96},{96,0},{1,33},{33,65},{65,97},{97,1},{2,34}... | collective-permute-start | bytes 786440 | tf_op jit(solution)/shard_map/ppermute | solution.py:254
  9.4 42.3 %collective-permute-start.2 = (bf16[2,64,1024]{2,1,0:T(8,128)(2,1)S(1)}, bf16[2,64,1024]{2,1,0:T(8,128)(2,1)S(1)}, u32[]{:S(2)}, u32[]{:S(2)}) collective-permute-start(bf16[2,64,1024]{2,1,0:T(8,128)(2,1)S(1)} %get-tuple-element.29), channel_id=1, source_target_pairs={{0,96},{32,0},{64,32},{96,64},{1,97},{33,1},{65,33},{97,65},{2,98}... | collective-permute-start | bytes 786440 | tf_op jit(solution)/shard_map/ppermute | solution.py:254

commit v6 on v5

--- a/solution.py
+++ b/solution.py
@@ -12,7 +12,7 @@
 TASK_PARAM = ("task", *PARAM)
 CHUNKS = (192, 64)
 SHIFTS = (2, 1, 3)
-GROUPS = (((2, 0, 256), (1, 0, 192), (3, 0, 192)), ((1, 192, 64), (3, 192, 64)))
+GROUPS = (((2, 0, 256),), ((1, 0, 192), (3, 0, 192)), ((1, 192, 64), (3, 192, 64)))
 GRAIN = 16
 OUT_ROWS = 64
 LANES = 128

time: 74.7 us -> 74.5 us (level)
  waiting for transfers between devices: 35.5 us -> 34 us
  Pallas kernels: 10 us -> 11 us
    ppermute x5, waiting for transfers between devices: 35.5 us -> 34 us  [shift(): lax.ppermute(value, axis, [(i, (i + by) % n) for i in range(n)])]
    pallas_call x3 -> x4, Pallas kernels: 4 us -> 4.91 us  [cut(): pl.pallas_call(functools.partial(cut_kernel, parts, pieces), in_specs=[pl...]
  transfers between devices with their start and end apart: 5 -> 5, of which waited for: 2 -> 2; matrix products, arithmetic and copies ran while one was open for 0% -> 0% of each run, Pallas kernels for 7% -> 9%
where the time goes in v6:
time: 74.5 us; the launch traced here: 74.2 us
  waiting for transfers between devices  34 us (46%)
  blocking collectives  19.8 us (27%)
  Pallas kernels  11 us (15%)
  starting transfers between devices  9.31 us (12%)
    ppermute x5, waiting for transfers between devices, shift(): lax.ppermute(value, axis, [(i, (i + by) % n) for i in range(n)])  34 us
    all_to_all x1, blocking collectives, shards(): gram = lax.all_to_all(gram, TASK_PARAM, 0, 0, tiled=True)  19.8 us
    ppermute x5, starting transfers between devices, shift(): lax.ppermute(value, axis, [(i, (i + by) % n) for i in range(n)])  9.31 us
    pallas_call x4, Pallas kernels, cut(): pl.pallas_call(functools.partial(cut_kernel, parts, pieces), in_specs=[pl...  4.91 us
    pallas_call x2, Pallas kernels, gram_of(): pl.pallas_call(functools.partial(gram_kernel, parts, per, rows, bases, fi...  3.93 us
    pallas_call x1, Pallas kernels, combine(): pl.pallas_call(functools.partial(combine_kernel, per, entries, tuple(layo...  2.11 us
  transfers between devices with their start and end apart: 5, of which 2 were waited for; matrix products, arithmetic and copies ran while one was open for 0% of the time, Pallas kernels for 9%

profile of v6, /device:TPU:1, one launch (start us, length us, event | category | flops | bytes accessed | tf_op | source)
XLA Modules:
  0.0 74.2 jit_solution(14759210903880083817)
XLA Ops:
  0.0 1.2 %cut.5 = bf16[2,256,1024]{2,1,0:T(8,128)(2,1)S(1)} custom-call(bf16[2,256,4096]{2,1,0:T(8,128)(2,1)} %grads_ref.7), custom_call_target="tpu_custom_call" | custom-call | tf_op jit(solution)/shard_map/cut/pallas_call | solution.py:236
  1.2 3.8 %collective-permute-start = (bf16[2,256,1024]{2,1,0:T(8,128)(2,1)S(1)}, bf16[2,256,1024]{2,1,0:T(8,128)(2,1)S(1)}, u32[]{:S(2)}, u32[]{:S(2)}) collective-permute-start(bf16[2,256,1024]{2,1,0:T(8,128)(2,1)S(1)} %cut.5), channel_id=1, source_target_pairs={{0,64},{32,96},{64,0},{96,32},{1,65},{33,97},{65,1},{97,33},{2,66}... | collective-permute-start | bytes 3145736 | tf_op jit(solution)/shard_map/ppermute | solution.py:254
  5.1 1.4 %cut.7 = (bf16[2,192,1024]{2,1,0:T(8,128)(2,1)S(1)}, bf16[2,192,1024]{2,1,0:T(8,128)(2,1)S(1)}) custom-call(bf16[2,256,4096]{2,1,0:T(8,128)(2,1)} %grads_ref.7), custom_call_target="tpu_custom_call" | custom-call | tf_op jit(solution)/shard_map/cut/pallas_call | solution.py:236
  6.5 0.5 collective-permute-start.3
  6.9 0.0 copy-start
  6.9 2.3 %collective-permute-start.4 = (bf16[2,192,1024]{2,1,0:T(8,128)(2,1)S(1)}, bf16[2,192,1024]{2,1,0:T(8,128)(2,1)S(1)}, u32[]{:S(2)}, u32[]{:S(2)}) collective-permute-start(bf16[2,192,1024]{2,1,0:T(8,128)(2,1)S(1)} %get-tuple-element.29), channel_id=1, source_target_pairs={{0,96},{32,0},{64,32},{96,64},{1,97},{33,1},{65,33},{97,65},{2,98}... | collective-permute-start | bytes 2359304 | tf_op jit(solution)/shard_map/ppermute | solution.py:254
  9.2 1.0 %cut.6 = (bf16[2,64,1024]{2,1,0:T(8,128)(2,1)S(1)}, bf16[2,64,1024]{2,1,0:T(8,128)(2,1)S(1)}) custom-call(bf16[2,256,4096]{2,1,0:T(8,128)(2,1)} %grads_ref.7), custom_call_target="tpu_custom_call" | custom-call | tf_op jit(solution)/shard_map/cut/pallas_call | solution.py:236
  10.3 0.1 collective-permute-start.1
  10.4 2.7 %collective-permute-start.2 = (bf16[2,64,1024]{2,1,0:T(8,128)(2,1)S(1)}, bf16[2,64,1024]{2,1,0:T(8,128)(2,1)S(1)}, u32[]{:S(2)}, u32[]{:S(2)}) collective-permute-start(bf16[2,64,1024]{2,1,0:T(8,128)(2,1)S(1)} %get-tuple-element.27), channel_id=1, source_target_pairs={{0,96},{32,0},{64,32},{96,64},{1,97},{33,1},{65,33},{97,65},{2,98}... | collective-permute-start | bytes 786440 | tf_op jit(solution)/shard_map/ppermute | solution.py:254
  13.0 1.2 %cut.4.refs_1_.refs_0_ = bf16[2,256,1024]{2,1,0:T(8,128)(2,1)S(1)} custom-call(bf16[2,256,4096]{2,1,0:T(8,128)(2,1)} %grads_ref.7), custom_call_target="tpu_custom_call" | custom-call | tf_op jit(solution)/shard_map/cut/pallas_call | solution.py:236
  14.3 31.3 %collective-permute-done.3.refs_3_.refs_2_ = bf16[2,192,1024]{2,1,0:T(8,128)(2,1)S(1)} collective-permute-done((bf16[2,192,1024]{2,1,0:T(8,128)(2,1)S(1)}, bf16[2,192,1024]{2,1,0:T(8,128)(2,1)S(1)}, u32[]{:S(2)}, u32[]{:S(2)}) %collective-permute-start.3) | collective-permute-done | bytes 786464 | tf_op jit(solution)/shard_map/ppermute | solution.py:254
  45.5 0.0 collective-permute-done.4.refs_4_.refs_3_
  45.5 0.0 collective-permute-done.refs_2_.refs_1_
  45.5 0.0 copy-done
  45.5 2.9 %gram.2 = (f32[512,128]{1,0:T(8,128)S(1)}, f32[8,128]{1,0:T(8,128)S(1)}, f32[128,128]{1,0:T(8,128)S(1)}, f32[8,8,128]{2,1,0:T(8,128)S(1)}) custom-call(s32[8]{0:T(128)S(1)} %copy-done, bf16[2,256,1024]{2,1,0:T(8,128)(2,1)S(1)} %cut.4.refs_1_.refs_0_, bf16[2,256,1024]{2,1,0:T(8,128)(2,1)S(1)} %collective-permute-done.refs_2_.refs_1_, ...), custom_call_target="tpu_custom_call" | custom-call | tf_op jit(solution)/shard_map/gram/pallas_call | solution.py:117
  48.5 2.7 %collective-permute-done.1.refs_2_.refs_4_ = bf16[2,64,1024]{2,1,0:T(8,128)(2,1)S(1)} collective-permute-done((bf16[2,64,1024]{2,1,0:T(8,128)(2,1)S(1)}, bf16[2,64,1024]{2,1,0:T(8,128)(2,1)S(1)}, u32[]{:S(2)}, u32[]{:S(2)}) %collective-permute-start.1) | collective-permute-done | bytes 262176 | tf_op jit(solution)/shard_map/ppermute | solution.py:254
  51.2 0.0 collective-permute-done.2.refs_3_.refs_5_
  51.2 1.0 %gram.3 = f32[128,128]{1,0:T(8,128)S(1)} custom-call(bf16[2,256,1024]{2,1,0:T(8,128)(2,1)S(1)} %cut.4.refs_1_.refs_0_, bf16[2,256,1024]{2,1,0:T(8,128)(2,1)S(1)} %collective-permute-done.refs_2_.refs_1_, bf16[2,64,1024]{2,1,0:T(8,128)(2,1)S(1)} %collective-permute-done.1.refs_2_.refs_4_, bf16[2,64,1024]{2,1,0:T(8,128)(2,1)S(1)} %collective-permute-done.2.refs_3_.refs_5_, ...), custom_call_target="tpu_custom_call" | custom-call | tf_op jit(solution)/shard_map/gram/pallas_call | solution.py:117
  52.2 19.8 %all_to_all.11 = f32[128,1,128]{2,1,0:T(1,128)S(1)} all-to-all(f32[128,1,128]{2,1,0:T(1,128)S(1)} %bitcast.9), channel_id=1, replica_groups=mesh['task'=4,'param_0'=4,'param_1'=4,'param_2'=2] {'task','param_0','pa..., dimensions={0} | all-to-all | bytes 131072 | tf_op jit(solution)/shard_map/all_to_all | solution.py:279
  72.0 2.1 %combine.1 = (f32[256,1024]{1,0:T(8,128)}, f32[128]{0:T(128)S(1)}, f32[128]{0:T(128)S(1)}) custom-call(f32[128,128]{1,0:T(8,128)S(1)} %bitcast.8, f32[8,128]{1,0:T(8,128)S(1)} %get-tuple-element.31.rows_ref, f32[128,128]{1,0:T(8,128)S(1)} %get-tuple-element.32.columns_ref, f32[8,8,128]{2,1,0:T(8,128)S(1)} %get-tuple-element.33.pick_ref, ...), custom_call_target="tpu_custom_call" | custom-call | tf_op jit(solution)/shard_map/combine/pallas_call | solution.py:201
  (1 shorter events, 0.0 us)
Async XLA Ops:
  1.2 44.3 %collective-permute-start = (bf16[2,256,1024]{2,1,0:T(8,128)(2,1)S(1)}, bf16[2,256,1024]{2,1,0:T(8,128)(2,1)S(1)}, u32[]{:S(2)}, u32[]{:S(2)}) collective-permute-start(bf16[2,256,1024]{2,1,0:T(8,128)(2,1)S(1)} %cut.5), channel_id=1, source_target_pairs={{0,64},{32,96},{64,0},{96,32},{1,65},{33,97},{65,1},{97,33},{2,66}... | collective-permute-start | bytes 3145736 | tf_op jit(solution)/shard_map/ppermute | solution.py:254
  6.5 39.1 %collective-permute-start.3 = (bf16[2,192,1024]{2,1,0:T(8,128)(2,1)S(1)}, bf16[2,192,1024]{2,1,0:T(8,128)(2,1)S(1)}, u32[]{:S(2)}, u32[]{:S(2)}) collective-permute-start(bf16[2,192,1024]{2,1,0:T(8,128)(2,1)S(1)} %get-tuple-element.28), channel_id=1, source_target_pairs={{0,32},{32,64},{64,96},{96,0},{1,33},{33,65},{65,97},{97,1},{2,34}... | collective-permute-start | bytes 2359304 | tf_op jit(solution)/shard_map/ppermute | solution.py:254
  6.9 38.6 %copy-start = (s32[8]{0:T(128)S(1)}, s32[8]{0:T(128)}, u32[]{:S(2)}) copy-start(s32[8]{0:T(128)} %refs_0_.1) | copy-start | bytes 100
  6.9 38.6 %collective-permute-start.4 = (bf16[2,192,1024]{2,1,0:T(8,128)(2,1)S(1)}, bf16[2,192,1024]{2,1,0:T(8,128)(2,1)S(1)}, u32[]{:S(2)}, u32[]{:S(2)}) collective-permute-start(bf16[2,192,1024]{2,1,0:T(8,128)(2,1)S(1)} %get-tuple-element.29), channel_id=1, source_target_pairs={{0,96},{32,0},{64,32},{96,64},{1,97},{33,1},{65,33},{97,65},{2,98}... | collective-permute-start | bytes 2359304 | tf_op jit(solution)/shard_map/ppermute | solution.py:254
  10.3 40.9 %collective-permute-start.1 = (bf16[2,64,1024]{2,1,0:T(8,128)(2,1)S(1)}, bf16[2,64,1024]{2,1,0:T(8,128)(2,1)S(1)}, u32[]{:S(2)}, u32[]{:S(2)}) collective-permute-start(bf16[2,64,1024]{2,1,0:T(8,128)(2,1)S(1)} %get-tuple-element.26), channel_id=1, source_target_pairs={{0,32},{32,64},{64,96},{96,0},{1,33},{33,65},{65,97},{97,1},{2,34}... | collective-permute-start | bytes 786440 | tf_op jit(solution)/shard_map/ppermute | solution.py:254
  10.4 40.8 %collective-permute-start.2 = (bf16[2,64,1024]{2,1,0:T(8,128)(2,1)S(1)}, bf16[2,64,1024]{2,1,0:T(8,128)(2,1)S(1)}, u32[]{:S(2)}, u32[]{:S(2)}) collective-permute-start(bf16[2,64,1024]{2,1,0:T(8,128)(2,1)S(1)} %get-tuple-element.27), channel_id=1, source_target_pairs={{0,96},{32,0},{64,32},{96,64},{1,97},{33,1},{65,33},{97,65},{2,98}... | collective-permute-start | bytes 786440 | tf_op jit(solution)/shard_map/ppermute | solution.py:254

commit v7 on v6

--- a/solution.py
+++ b/solution.py
@@ -10,9 +10,9 @@
 
 PARAM = ("param_0", "param_1", "param_2")
 TASK_PARAM = ("task", *PARAM)
-CHUNKS = (192, 64)
+CHUNKS = (208, 48)
 SHIFTS = (2, 1, 3)
-GROUPS = (((2, 0, 256),), ((1, 0, 192), (3, 0, 192)), ((1, 192, 64), (3, 192, 64)))
+GROUPS = (((2, 0, 256), (1, 0, 208), (3, 0, 208)), ((1, 208, 48), (3, 208, 48)))
 GRAIN = 16
 OUT_ROWS = 64
 LANES = 128
@@ -163,6 +163,7 @@
     for row0, size, places_of in chunks:
         blocks = [(refs[k], base) for k, base in places_of]
         for top in range(0, size, OUT_ROWS):
+            here = min(OUT_ROWS, size - top)
 
             def body(r, _):
                 at = pl.multiple_of(top + r * GRAIN, GRAIN)
@@ -177,8 +178,8 @@
                     total_ref[pl.ds(row0 + at, GRAIN), cols] = total
                 return 0
 
-            lax.fori_loop(0, OUT_ROWS // GRAIN, body, 0)
-            span = pl.ds(row0 + top, OUT_ROWS)
+            lax.fori_loop(0, here // GRAIN, body, 0)
+            span = pl.ds(row0 + top, here)
             copy = pltpu.make_async_copy(total_ref.at[span], out_ref.at[span], sems.at[len(copies)])
             copy.start()
             copies.append(copy)
@@ -209,7 +210,7 @@
         ],
         scratch_shapes=[
             pltpu.VMEM((row0, width), jnp.float32),
-            pltpu.SemaphoreType.DMA((row0 // OUT_ROWS,)),
+            pltpu.SemaphoreType.DMA((sum(-(-size // OUT_ROWS) for size in sizes),)),
         ],
         compiler_params=pltpu.CompilerParams(vmem_limit_bytes=4 << 20),
         name="combine",

time: 74.5 us -> 74.5 us (level)
  waiting for transfers between devices: 34 us -> 35.3 us
  Pallas kernels: 11 us -> 10 us
    ppermute x5, waiting for transfers between devices: 34 us -> 35.3 us  [shift(): lax.ppermute(value, axis, [(i, (i + by) % n) for i in range(n)])]
    pallas_call x4 -> x3, Pallas kernels: 4.91 us -> 4.04 us  [cut(): pl.pallas_call(functools.partial(cut_kernel, parts, pieces), in_specs=[pl...]
  transfers between devices with their start and end apart: 5 -> 5, of which waited for: 2 -> 2; matrix products, arithmetic and copies ran while one was open for 0% -> 0% of each run, Pallas kernels for 9% -> 7%
where the time goes in v7:
time: 74.5 us; the launch traced here: 74.3 us
  waiting for transfers between devices  35.3 us (47%)
  blocking collectives  19.7 us (26%)
  Pallas kernels  10 us (13%)
  starting transfers between devices  9.24 us (12%)
    ppermute x5, waiting for transfers between devices, shift(): lax.ppermute(value, axis, [(i, (i + by) % n) for i in range(n)])  35.3 us
    all_to_all x1, blocking collectives, shards(): gram = lax.all_to_all(gram, TASK_PARAM, 0, 0, tiled=True)  19.7 us
    ppermute x5, starting transfers between devices, shift(): lax.ppermute(value, axis, [(i, (i + by) % n) for i in range(n)])  9.24 us
    pallas_call x3, Pallas kernels, cut(): pl.pallas_call(functools.partial(cut_kernel, parts, pieces), in_specs=[pl...  4.04 us
    pallas_call x2, Pallas kernels, gram_of(): pl.pallas_call(functools.partial(gram_kernel, parts, per, rows, bases, fi...  3.93 us
    pallas_call x1, Pallas kernels, combine(): pl.pallas_call(functools.partial(combine_kernel, per, entries, tuple(layo...  2.08 us
  transfers between devices with their start and end apart: 5, of which 2 were waited for; matrix products, arithmetic and copies ran while one was open for 0% of the time, Pallas kernels for 7%

profile of v7, /device:TPU:1, one launch (start us, length us, event | category | flops | bytes accessed | tf_op | source)
XLA Modules:
  0.0 74.3 jit_solution(639080984048269108)
XLA Ops:
  0.0 1.8 %cut.4 = (bf16[2,256,1024]{2,1,0:T(8,128)(2,1)S(1)}, bf16[2,208,1024]{2,1,0:T(8,128)(2,1)S(1)}, bf16[2,208,1024]{2,1,0:T(8,128)(2,1)S(1)}) custom-call(bf16[2,256,4096]{2,1,0:T(8,128)(2,1)} %grads_ref.5), custom_call_target="tpu_custom_call" | custom-call | tf_op jit(solution)/shard_map/cut/pallas_call | solution.py:237
  1.8 3.8 %collective-permute-start = (bf16[2,256,1024]{2,1,0:T(8,128)(2,1)S(1)}, bf16[2,256,1024]{2,1,0:T(8,128)(2,1)S(1)}, u32[]{:S(2)}, u32[]{:S(2)}) collective-permute-start(bf16[2,256,1024]{2,1,0:T(8,128)(2,1)S(1)} %get-tuple-element.27), channel_id=1, source_target_pairs={{0,64},{32,96},{64,0},{96,32},{1,65},{33,97},{65,1},{97,33},{2,66}... | collective-permute-start | bytes 3145736 | tf_op jit(solution)/shard_map/ppermute | solution.py:255
  5.6 0.4 collective-permute-start.3
  6.0 0.0 copy-start
  6.0 2.3 %collective-permute-start.4 = (bf16[2,208,1024]{2,1,0:T(8,128)(2,1)S(1)}, bf16[2,208,1024]{2,1,0:T(8,128)(2,1)S(1)}, u32[]{:S(2)}, u32[]{:S(2)}) collective-permute-start(bf16[2,208,1024]{2,1,0:T(8,128)(2,1)S(1)} %get-tuple-element.31), channel_id=1, source_target_pairs={{0,96},{32,0},{64,32},{96,64},{1,97},{33,1},{65,33},{97,65},{2,98}... | collective-permute-start | bytes 2555912 | tf_op jit(solution)/shard_map/ppermute | solution.py:255
  8.3 1.0 %cut.5 = (bf16[2,48,1024]{2,1,0:T(8,128)(2,1)S(1)}, bf16[2,48,1024]{2,1,0:T(8,128)(2,1)S(1)}) custom-call(bf16[2,256,4096]{2,1,0:T(8,128)(2,1)} %grads_ref.5), custom_call_target="tpu_custom_call" | custom-call | tf_op jit(solution)/shard_map/cut/pallas_call | solution.py:237
  9.3 0.1 collective-permute-start.1
  9.4 2.7 %collective-permute-start.2 = (bf16[2,48,1024]{2,1,0:T(8,128)(2,1)S(1)}, bf16[2,48,1024]{2,1,0:T(8,128)(2,1)S(1)}, u32[]{:S(2)}, u32[]{:S(2)}) collective-permute-start(bf16[2,48,1024]{2,1,0:T(8,128)(2,1)S(1)} %get-tuple-element.29), channel_id=1, source_target_pairs={{0,96},{32,0},{64,32},{96,64},{1,97},{33,1},{65,33},{97,65},{2,98}... | collective-permute-start | bytes 589832 | tf_op jit(solution)/shard_map/ppermute | solution.py:255
  12.1 1.2 %cut.3.refs_1_.refs_0_ = bf16[2,256,1024]{2,1,0:T(8,128)(2,1)S(1)} custom-call(bf16[2,256,4096]{2,1,0:T(8,128)(2,1)} %grads_ref.5), custom_call_target="tpu_custom_call" | custom-call | tf_op jit(solution)/shard_map/cut/pallas_call | solution.py:237
  13.3 34.2 %collective-permute-done.3.refs_3_.refs_2_ = bf16[2,208,1024]{2,1,0:T(8,128)(2,1)S(1)} collective-permute-done((bf16[2,208,1024]{2,1,0:T(8,128)(2,1)S(1)}, bf16[2,208,1024]{2,1,0:T(8,128)(2,1)S(1)}, u32[]{:S(2)}, u32[]{:S(2)}) %collective-permute-start.3) | collective-permute-done | bytes 852000 | tf_op jit(solution)/shard_map/ppermute | solution.py:255
  47.5 0.0 collective-permute-done.4.refs_4_.refs_3_
  47.5 0.0 collective-permute-done.refs_2_.refs_1_
  47.5 0.0 copy-done
  47.5 3.1 %gram.2 = (f32[512,128]{1,0:T(8,128)S(1)}, f32[8,128]{1,0:T(8,128)S(1)}, f32[128,128]{1,0:T(8,128)S(1)}, f32[8,8,128]{2,1,0:T(8,128)S(1)}) custom-call(s32[8]{0:T(128)S(1)} %copy-done, bf16[2,256,1024]{2,1,0:T(8,128)(2,1)S(1)} %cut.3.refs_1_.refs_0_, bf16[2,256,1024]{2,1,0:T(8,128)(2,1)S(1)} %collective-permute-done.refs_2_.refs_1_, ...), custom_call_target="tpu_custom_call" | custom-call | tf_op jit(solution)/shard_map/gram/pallas_call | solution.py:117
  50.6 1.1 %collective-permute-done.1.refs_2_.refs_4_ = bf16[2,48,1024]{2,1,0:T(8,128)(2,1)S(1)} collective-permute-done((bf16[2,48,1024]{2,1,0:T(8,128)(2,1)S(1)}, bf16[2,48,1024]{2,1,0:T(8,128)(2,1)S(1)}, u32[]{:S(2)}, u32[]{:S(2)}) %collective-permute-start.1) | collective-permute-done | bytes 196640 | tf_op jit(solution)/shard_map/ppermute | solution.py:255
  51.7 0.0 collective-permute-done.2.refs_3_.refs_5_
  51.7 0.8 %gram.3 = f32[128,128]{1,0:T(8,128)S(1)} custom-call(bf16[2,256,1024]{2,1,0:T(8,128)(2,1)S(1)} %cut.3.refs_1_.refs_0_, bf16[2,256,1024]{2,1,0:T(8,128)(2,1)S(1)} %collective-permute-done.refs_2_.refs_1_, bf16[2,48,1024]{2,1,0:T(8,128)(2,1)S(1)} %collective-permute-done.1.refs_2_.refs_4_, bf16[2,48,1024]{2,1,0:T(8,128)(2,1)S(1)} %collective-permute-done.2.refs_3_.refs_5_, ...), custom_call_target="tpu_custom_call" | custom-call | tf_op jit(solution)/shard_map/gram/pallas_call | solution.py:117
  52.5 19.7 %all_to_all.11 = f32[128,1,128]{2,1,0:T(1,128)S(1)} all-to-all(f32[128,1,128]{2,1,0:T(1,128)S(1)} %bitcast.9), channel_id=1, replica_groups=mesh['task'=4,'param_0'=4,'param_1'=4,'param_2'=2] {'task','param_0','pa..., dimensions={0} | all-to-all | bytes 131072 | tf_op jit(solution)/shard_map/all_to_all | solution.py:280
  72.2 2.1 %combine.1 = (f32[256,1024]{1,0:T(8,128)}, f32[128]{0:T(128)S(1)}, f32[128]{0:T(128)S(1)}) custom-call(f32[128,128]{1,0:T(8,128)S(1)} %bitcast.8, f32[8,128]{1,0:T(8,128)S(1)} %get-tuple-element.33.rows_ref, f32[128,128]{1,0:T(8,128)S(1)} %get-tuple-element.34.columns_ref, f32[8,8,128]{2,1,0:T(8,128)S(1)} %get-tuple-element.35.pick_ref, ...), custom_call_target="tpu_custom_call" | custom-call | tf_op jit(solution)/shard_map/combine/pallas_call | solution.py:202
  (1 shorter events, 0.0 us)
Async XLA Ops:
  1.8 45.7 %collective-permute-start = (bf16[2,256,1024]{2,1,0:T(8,128)(2,1)S(1)}, bf16[2,256,1024]{2,1,0:T(8,128)(2,1)S(1)}, u32[]{:S(2)}, u32[]{:S(2)}) collective-permute-start(bf16[2,256,1024]{2,1,0:T(8,128)(2,1)S(1)} %get-tuple-element.27), channel_id=1, source_target_pairs={{0,64},{32,96},{64,0},{96,32},{1,65},{33,97},{65,1},{97,33},{2,66}... | collective-permute-start | bytes 3145736 | tf_op jit(solution)/shard_map/ppermute | solution.py:255
  5.6 41.9 %collective-permute-start.3 = (bf16[2,208,1024]{2,1,0:T(8,128)(2,1)S(1)}, bf16[2,208,1024]{2,1,0:T(8,128)(2,1)S(1)}, u32[]{:S(2)}, u32[]{:S(2)}) collective-permute-start(bf16[2,208,1024]{2,1,0:T(8,128)(2,1)S(1)} %get-tuple-element.30), channel_id=1, source_target_pairs={{0,32},{32,64},{64,96},{96,0},{1,33},{33,65},{65,97},{97,1},{2,34}... | collective-permute-start | bytes 2555912 | tf_op jit(solution)/shard_map/ppermute | solution.py:255
  6.0 41.5 %copy-start = (s32[8]{0:T(128)S(1)}, s32[8]{0:T(128)}, u32[]{:S(2)}) copy-start(s32[8]{0:T(128)} %refs_0_.1) | copy-start | bytes 100
  6.0 41.5 %collective-permute-start.4 = (bf16[2,208,1024]{2,1,0:T(8,128)(2,1)S(1)}, bf16[2,208,1024]{2,1,0:T(8,128)(2,1)S(1)}, u32[]{:S(2)}, u32[]{:S(2)}) collective-permute-start(bf16[2,208,1024]{2,1,0:T(8,128)(2,1)S(1)} %get-tuple-element.31), channel_id=1, source_target_pairs={{0,96},{32,0},{64,32},{96,64},{1,97},{33,1},{65,33},{97,65},{2,98}... | collective-permute-start | bytes 2555912 | tf_op jit(solution)/shard_map/ppermute | solution.py:255
  9.3 42.4 %collective-permute-start.1 = (bf16[2,48,1024]{2,1,0:T(8,128)(2,1)S(1)}, bf16[2,48,1024]{2,1,0:T(8,128)(2,1)S(1)}, u32[]{:S(2)}, u32[]{:S(2)}) collective-permute-start(bf16[2,48,1024]{2,1,0:T(8,128)(2,1)S(1)} %get-tuple-element.28), channel_id=1, source_target_pairs={{0,32},{32,64},{64,96},{96,0},{1,33},{33,65},{65,97},{97,1},{2,34}... | collective-permute-start | bytes 589832 | tf_op jit(solution)/shard_map/ppermute | solution.py:255
  9.4 42.3 %collective-permute-start.2 = (bf16[2,48,1024]{2,1,0:T(8,128)(2,1)S(1)}, bf16[2,48,1024]{2,1,0:T(8,128)(2,1)S(1)}, u32[]{:S(2)}, u32[]{:S(2)}) collective-permute-start(bf16[2,48,1024]{2,1,0:T(8,128)(2,1)S(1)} %get-tuple-element.29), channel_id=1, source_target_pairs={{0,96},{32,0},{64,32},{96,64},{1,97},{33,1},{65,33},{97,65},{2,98}... | collective-permute-start | bytes 589832 | tf_op jit(solution)/shard_map/ppermute | solution.py:255

commit v8 on v7

--- a/solution.py
+++ b/solution.py
@@ -12,7 +12,7 @@
 TASK_PARAM = ("task", *PARAM)
 CHUNKS = (208, 48)
 SHIFTS = (2, 1, 3)
-GROUPS = (((2, 0, 256), (1, 0, 208), (3, 0, 208)), ((1, 208, 48), (3, 208, 48)))
+GROUPS = (((2, 0, 256),), ((1, 0, 208), (3, 0, 208)), ((1, 208, 48), (3, 208, 48)))
 GRAIN = 16
 OUT_ROWS = 64
 LANES = 128

time: 74.5 us -> 74.2 us (level)
  waiting for transfers between devices: 35.3 us -> 33.8 us
  Pallas kernels: 10 us -> 11 us
    ppermute x5, waiting for transfers between devices: 35.3 us -> 33.8 us  [shift(): lax.ppermute(value, axis, [(i, (i + by) % n) for i in range(n)])]
    pallas_call x3 -> x4, Pallas kernels: 4.04 us -> 4.94 us  [cut(): pl.pallas_call(functools.partial(cut_kernel, parts, pieces), in_specs=[pl...]
  transfers between devices with their start and end apart: 5 -> 5, of which waited for: 2 -> 2; matrix products, arithmetic and copies ran while one was open for 0% -> 0% of each run, Pallas kernels for 7% -> 9%
where the time goes in v8:
time: 74.2 us; the launch traced here: 74 us
  waiting for transfers between devices  33.8 us (46%)
  blocking collectives  19.8 us (27%)
  Pallas kernels  11 us (15%)
  starting transfers between devices  9.31 us (13%)
    ppermute x5, waiting for transfers between devices, shift(): lax.ppermute(value, axis, [(i, (i + by) % n) for i in range(n)])  33.8 us
    all_to_all x1, blocking collectives, shards(): gram = lax.all_to_all(gram, TASK_PARAM, 0, 0, tiled=True)  19.8 us
    ppermute x5, starting transfers between devices, shift(): lax.ppermute(value, axis, [(i, (i + by) % n) for i in range(n)])  9.31 us
    pallas_call x4, Pallas kernels, cut(): pl.pallas_call(functools.partial(cut_kernel, parts, pieces), in_specs=[pl...  4.94 us
    pallas_call x2, Pallas kernels, gram_of(): pl.pallas_call(functools.partial(gram_kernel, parts, per, rows, bases, fi...  3.93 us
    pallas_call x1, Pallas kernels, combine(): pl.pallas_call(functools.partial(combine_kernel, per, entries, tuple(layo...  2.08 us
  transfers between devices with their start and end apart: 5, of which 2 were waited for; matrix products, arithmetic and copies ran while one was open for 0% of the time, Pallas kernels for 9%

profile of v8, /device:TPU:1, one launch (start us, length us, event | category | flops | bytes accessed | tf_op | source)
XLA Modules:
  0.0 74.0 jit_solution(16395245845079273453)
XLA Ops:
  0.0 1.2 %cut.5 = bf16[2,256,1024]{2,1,0:T(8,128)(2,1)S(1)} custom-call(bf16[2,256,4096]{2,1,0:T(8,128)(2,1)} %grads_ref.7), custom_call_target="tpu_custom_call" | custom-call | tf_op jit(solution)/shard_map/cut/pallas_call | solution.py:237
  1.2 3.8 %collective-permute-start = (bf16[2,256,1024]{2,1,0:T(8,128)(2,1)S(1)}, bf16[2,256,1024]{2,1,0:T(8,128)(2,1)S(1)}, u32[]{:S(2)}, u32[]{:S(2)}) collective-permute-start(bf16[2,256,1024]{2,1,0:T(8,128)(2,1)S(1)} %cut.5), channel_id=1, source_target_pairs={{0,64},{32,96},{64,0},{96,32},{1,65},{33,97},{65,1},{97,33},{2,66}... | collective-permute-start | bytes 3145736 | tf_op jit(solution)/shard_map/ppermute | solution.py:255
  5.1 1.4 %cut.7 = (bf16[2,208,1024]{2,1,0:T(8,128)(2,1)S(1)}, bf16[2,208,1024]{2,1,0:T(8,128)(2,1)S(1)}) custom-call(bf16[2,256,4096]{2,1,0:T(8,128)(2,1)} %grads_ref.7), custom_call_target="tpu_custom_call" | custom-call | tf_op jit(solution)/shard_map/cut/pallas_call | solution.py:237
  6.5 0.5 collective-permute-start.3
  7.0 0.0 copy-start
  7.0 2.3 %collective-permute-start.4 = (bf16[2,208,1024]{2,1,0:T(8,128)(2,1)S(1)}, bf16[2,208,1024]{2,1,0:T(8,128)(2,1)S(1)}, u32[]{:S(2)}, u32[]{:S(2)}) collective-permute-start(bf16[2,208,1024]{2,1,0:T(8,128)(2,1)S(1)} %get-tuple-element.29), channel_id=1, source_target_pairs={{0,96},{32,0},{64,32},{96,64},{1,97},{33,1},{65,33},{97,65},{2,98}... | collective-permute-start | bytes 2555912 | tf_op jit(solution)/shard_map/ppermute | solution.py:255
  9.3 1.0 %cut.6 = (bf16[2,48,1024]{2,1,0:T(8,128)(2,1)S(1)}, bf16[2,48,1024]{2,1,0:T(8,128)(2,1)S(1)}) custom-call(bf16[2,256,4096]{2,1,0:T(8,128)(2,1)} %grads_ref.7), custom_call_target="tpu_custom_call" | custom-call | tf_op jit(solution)/shard_map/cut/pallas_call | solution.py:237
  10.3 0.1 collective-permute-start.1
  10.4 2.7 %collective-permute-start.2 = (bf16[2,48,1024]{2,1,0:T(8,128)(2,1)S(1)}, bf16[2,48,1024]{2,1,0:T(8,128)(2,1)S(1)}, u32[]{:S(2)}, u32[]{:S(2)}) collective-permute-start(bf16[2,48,1024]{2,1,0:T(8,128)(2,1)S(1)} %get-tuple-element.27), channel_id=1, source_target_pairs={{0,96},{32,0},{64,32},{96,64},{1,97},{33,1},{65,33},{97,65},{2,98}... | collective-permute-start | bytes 589832 | tf_op jit(solution)/shard_map/ppermute | solution.py:255
  13.1 1.2 %cut.4.refs_1_.refs_0_ = bf16[2,256,1024]{2,1,0:T(8,128)(2,1)S(1)} custom-call(bf16[2,256,4096]{2,1,0:T(8,128)(2,1)} %grads_ref.7), custom_call_target="tpu_custom_call" | custom-call | tf_op jit(solution)/shard_map/cut/pallas_call | solution.py:237
  14.3 32.6 %collective-permute-done.3.refs_3_.refs_2_ = bf16[2,208,1024]{2,1,0:T(8,128)(2,1)S(1)} collective-permute-done((bf16[2,208,1024]{2,1,0:T(8,128)(2,1)S(1)}, bf16[2,208,1024]{2,1,0:T(8,128)(2,1)S(1)}, u32[]{:S(2)}, u32[]{:S(2)}) %collective-permute-start.3) | collective-permute-done | bytes 852000 | tf_op jit(solution)/shard_map/ppermute | solution.py:255
  46.9 0.0 collective-permute-done.4.refs_4_.refs_3_
  46.9 0.0 collective-permute-done.refs_2_.refs_1_
  46.9 0.0 copy-done
  47.0 3.1 %gram.2 = (f32[512,128]{1,0:T(8,128)S(1)}, f32[8,128]{1,0:T(8,128)S(1)}, f32[128,128]{1,0:T(8,128)S(1)}, f32[8,8,128]{2,1,0:T(8,128)S(1)}) custom-call(s32[8]{0:T(128)S(1)} %copy-done, bf16[2,256,1024]{2,1,0:T(8,128)(2,1)S(1)} %cut.4.refs_1_.refs_0_, bf16[2,256,1024]{2,1,0:T(8,128)(2,1)S(1)} %collective-permute-done.refs_2_.refs_1_, ...), custom_call_target="tpu_custom_call" | custom-call | tf_op jit(solution)/shard_map/gram/pallas_call | solution.py:117
  50.0 1.1 %collective-permute-done.1.refs_2_.refs_4_ = bf16[2,48,1024]{2,1,0:T(8,128)(2,1)S(1)} collective-permute-done((bf16[2,48,1024]{2,1,0:T(8,128)(2,1)S(1)}, bf16[2,48,1024]{2,1,0:T(8,128)(2,1)S(1)}, u32[]{:S(2)}, u32[]{:S(2)}) %collective-permute-start.1) | collective-permute-done | bytes 196640 | tf_op jit(solution)/shard_map/ppermute | solution.py:255
  51.2 0.0 collective-permute-done.2.refs_3_.refs_5_
  51.2 0.9 %gram.3 = f32[128,128]{1,0:T(8,128)S(1)} custom-call(bf16[2,256,1024]{2,1,0:T(8,128)(2,1)S(1)} %cut.4.refs_1_.refs_0_, bf16[2,256,1024]{2,1,0:T(8,128)(2,1)S(1)} %collective-permute-done.refs_2_.refs_1_, bf16[2,48,1024]{2,1,0:T(8,128)(2,1)S(1)} %collective-permute-done.1.refs_2_.refs_4_, bf16[2,48,1024]{2,1,0:T(8,128)(2,1)S(1)} %collective-permute-done.2.refs_3_.refs_5_, ...), custom_call_target="tpu_custom_call" | custom-call | tf_op jit(solution)/shard_map/gram/pallas_call | solution.py:117
  52.0 19.8 %all_to_all.11 = f32[128,1,128]{2,1,0:T(1,128)S(1)} all-to-all(f32[128,1,128]{2,1,0:T(1,128)S(1)} %bitcast.9), channel_id=1, replica_groups=mesh['task'=4,'param_0'=4,'param_1'=4,'param_2'=2] {'task','param_0','pa..., dimensions={0} | all-to-all | bytes 131072 | tf_op jit(solution)/shard_map/all_to_all | solution.py:280
  71.9 2.1 %combine.1 = (f32[256,1024]{1,0:T(8,128)}, f32[128]{0:T(128)S(1)}, f32[128]{0:T(128)S(1)}) custom-call(f32[128,128]{1,0:T(8,128)S(1)} %bitcast.8, f32[8,128]{1,0:T(8,128)S(1)} %get-tuple-element.31.rows_ref, f32[128,128]{1,0:T(8,128)S(1)} %get-tuple-element.32.columns_ref, f32[8,8,128]{2,1,0:T(8,128)S(1)} %get-tuple-element.33.pick_ref, ...), custom_call_target="tpu_custom_call" | custom-call | tf_op jit(solution)/shard_map/combine/pallas_call | solution.py:202
  (1 shorter events, 0.0 us)
Async XLA Ops:
  1.2 45.7 %collective-permute-start = (bf16[2,256,1024]{2,1,0:T(8,128)(2,1)S(1)}, bf16[2,256,1024]{2,1,0:T(8,128)(2,1)S(1)}, u32[]{:S(2)}, u32[]{:S(2)}) collective-permute-start(bf16[2,256,1024]{2,1,0:T(8,128)(2,1)S(1)} %cut.5), channel_id=1, source_target_pairs={{0,64},{32,96},{64,0},{96,32},{1,65},{33,97},{65,1},{97,33},{2,66}... | collective-permute-start | bytes 3145736 | tf_op jit(solution)/shard_map/ppermute | solution.py:255
  6.5 40.4 %collective-permute-start.3 = (bf16[2,208,1024]{2,1,0:T(8,128)(2,1)S(1)}, bf16[2,208,1024]{2,1,0:T(8,128)(2,1)S(1)}, u32[]{:S(2)}, u32[]{:S(2)}) collective-permute-start(bf16[2,208,1024]{2,1,0:T(8,128)(2,1)S(1)} %get-tuple-element.28), channel_id=1, source_target_pairs={{0,32},{32,64},{64,96},{96,0},{1,33},{33,65},{65,97},{97,1},{2,34}... | collective-permute-start | bytes 2555912 | tf_op jit(solution)/shard_map/ppermute | solution.py:255
  7.0 40.0 %copy-start = (s32[8]{0:T(128)S(1)}, s32[8]{0:T(128)}, u32[]{:S(2)}) copy-start(s32[8]{0:T(128)} %refs_0_.1) | copy-start | bytes 100
  7.0 40.0 %collective-permute-start.4 = (bf16[2,208,1024]{2,1,0:T(8,128)(2,1)S(1)}, bf16[2,208,1024]{2,1,0:T(8,128)(2,1)S(1)}, u32[]{:S(2)}, u32[]{:S(2)}) collective-permute-start(bf16[2,208,1024]{2,1,0:T(8,128)(2,1)S(1)} %get-tuple-element.29), channel_id=1, source_target_pairs={{0,96},{32,0},{64,32},{96,64},{1,97},{33,1},{65,33},{97,65},{2,98}... | collective-permute-start | bytes 2555912 | tf_op jit(solution)/shard_map/ppermute | solution.py:255
  10.3 40.8 %collective-permute-start.1 = (bf16[2,48,1024]{2,1,0:T(8,128)(2,1)S(1)}, bf16[2,48,1024]{2,1,0:T(8,128)(2,1)S(1)}, u32[]{:S(2)}, u32[]{:S(2)}) collective-permute-start(bf16[2,48,1024]{2,1,0:T(8,128)(2,1)S(1)} %get-tuple-element.26), channel_id=1, source_target_pairs={{0,32},{32,64},{64,96},{96,0},{1,33},{33,65},{65,97},{97,1},{2,34}... | collective-permute-start | bytes 589832 | tf_op jit(solution)/shard_map/ppermute | solution.py:255
  10.4 40.8 %collective-permute-start.2 = (bf16[2,48,1024]{2,1,0:T(8,128)(2,1)S(1)}, bf16[2,48,1024]{2,1,0:T(8,128)(2,1)S(1)}, u32[]{:S(2)}, u32[]{:S(2)}) collective-permute-start(bf16[2,48,1024]{2,1,0:T(8,128)(2,1)S(1)} %get-tuple-element.27), channel_id=1, source_target_pairs={{0,96},{32,0},{64,32},{96,64},{1,97},{33,1},{65,33},{97,65},{2,98}... | collective-permute-start | bytes 589832 | tf_op jit(solution)/shard_map/ppermute | solution.py:255
